TPU v7x, 512 devices: a whole 4x8x8 slice. The times are simulated.
512 devices in a mesh: src: 16 (over y, x_hi), space: 32 (over x_lo, z, core).
Axes of the slice: x: 4 (x_hi: 2, x_lo: 2; x = x_hi * 2 + x_lo), y: 8, z: 8, core: 2. Of those that a mesh axis runs over, the one named last changes fastest.
Arguments:
- velocity: float32 [32, 512, 256], P('space'), may hold values from 0.5 to 2
- station_cells: int32 [16, 3], P('src'), may hold values from 0 to 511, as said below
- event_cells: int32 [3, 8192], replicated, may hold values from 0 to 511, as said below
- delays: float32 [16, 8192], P('src'), may hold values from -6 to 6
- active: int32 [2, 16, 32, 16], P(None, 'src', 'space'), may hold values from 0 to 1, as said below
Outputs:
- traveltimes: float32 [16, 32, 512, 256], P('src', 'space')
- kernel: float32 [32, 512, 256], P('space', 'src')
Inputs may be any that keep to these rules, and one draw needn't show every extreme that they name: `station_cells`: stations lie in the top four layers: third coordinate below 4, first below 32, second below 512. `event_cells`: row 0 holds first coordinates below 32, row 1 second ones below 512, row 2 third ones below 256. `active`: 1 marks a tile whose cells are updated in that round for that station.
All inputs are finite; a program needn't handle non-finite values.
Results may differ from a plain program's by a relative error of at most 0.0003.
Values sent between devices are 32-bit elements; how exact they have to be, the bound alone decides.
A program may use at most 64 MiB of HBM per device.

v0:
```python
import jax
import jax.numpy as jnp
from jax import lax
from jax.sharding import PartitionSpec as P

TY = 32
ROUNDS = 2
SWEEPS = 2
ADJ_SWEEPS = 4


BIG = 1000000.0


def padded(array, sides, width):
    for axis, dim in sides:
        size, length = (lax.axis_size(axis), array.shape[dim])
        up = [(i, (i + 1) % size) for i in range(size - 1)]
        down = [(j, i) for i, j in up]
        last = lax.slice_in_dim(array, length - width, length, axis=dim)
        first = lax.slice_in_dim(array, 0, width, axis=dim)
        before = lax.ppermute(last, axis, up)
        after = lax.ppermute(first, axis, down)
        array = jnp.concatenate([before, array, after], axis=dim)
    return array


def godunov(near_x, near_y, near_z, cost_cell):
    lowest = jnp.minimum(jnp.minimum(near_x, near_y), near_z)
    highest = jnp.maximum(jnp.maximum(near_x, near_y), near_z)
    middle = jnp.maximum(
        jnp.minimum(near_x, near_y), jnp.minimum(jnp.maximum(near_x, near_y), near_z)
    )
    first_gap = middle - lowest
    second_gap = highest - lowest
    single = lowest + cost_cell
    double = lowest + 0.5 * (
        first_gap + jnp.sqrt(jnp.maximum(2.0 * cost_cell * cost_cell - first_gap * first_gap, 0.0))
    )
    gaps = first_gap + second_gap
    triple = (
        lowest
        + (
            gaps
            + jnp.sqrt(
                jnp.maximum(
                    gaps * gaps
                    - 3.0
                    * (first_gap * first_gap + second_gap * second_gap - cost_cell * cost_cell),
                    0.0,
                )
            )
        )
        / 3.0
    )
    return jnp.where(single <= middle, single, jnp.where(double <= highest, double, triple))


def end_slab(field, axis_index, fill):
    return jnp.full_like(lax.slice_in_dim(field, 0, 1, axis=axis_index), fill)


def shifted(field, axis_index, low_rim, high_rim):
    length = field.shape[axis_index]
    before = jnp.concatenate(
        [low_rim, lax.slice_in_dim(field, 0, length - 1, axis=axis_index)], axis=axis_index
    )
    after = jnp.concatenate(
        [lax.slice_in_dim(field, 1, length, axis=axis_index), high_rim], axis=axis_index
    )
    return (before, after)


def six_neighbours(field, low_rim, high_rim, fill):
    x_before, x_after = shifted(field, 1, low_rim, high_rim)
    y_before, y_after = shifted(field, 2, end_slab(field, 2, fill), end_slab(field, 2, fill))
    z_before, z_after = shifted(field, 3, end_slab(field, 3, fill), end_slab(field, 3, fill))
    return [x_before, x_after, y_before, y_after, z_before, z_after]


def outer_rims(extended):
    position = lax.axis_index("space")
    final_index = lax.axis_size("space") - 1
    low_rim = jnp.where(position == 0, BIG, extended[:, :1])
    high_rim = jnp.where(position == final_index, BIG, extended[:, -1:])
    return (low_rim, high_rim)


def sweep_once(times, slowness, tile_mask, station_mask):
    extended = padded(times, (("space", 1),), 1)
    low_rim, high_rim = outer_rims(extended)
    beside_all = six_neighbours(times, low_rim, high_rim, BIG)
    update = godunov(
        jnp.minimum(beside_all[0], beside_all[1]),
        jnp.minimum(beside_all[2], beside_all[3]),
        jnp.minimum(beside_all[4], beside_all[5]),
        slowness[None],
    )
    station_count, rows_x, rows_y, rows_z = times.shape
    tile_count = rows_y // TY
    shape_tiles = (station_count, rows_x, tile_count, TY, rows_z)
    chosen = jnp.where(tile_mask, update.reshape(shape_tiles), times.reshape(shape_tiles)).reshape(
        times.shape
    )
    return jnp.where(station_mask, 0.0, chosen)


def smooth_along(extended, axis_index):
    length = extended.shape[axis_index]
    first = lax.slice_in_dim(extended, 0, length - 2, axis=axis_index)
    centre = lax.slice_in_dim(extended, 1, length - 1, axis=axis_index)
    after = lax.slice_in_dim(extended, 2, length, axis=axis_index)
    return (first + 2.0 * centre + after) * 0.25


def pad_zero(field, axis_index):
    widths = [(0, 0)] * field.ndim
    widths[axis_index] = (1, 1)
    return jnp.pad(field, widths)


def per_device(velocity, station_cells, event_cells, delays, active):
    slowness = 1.0 / velocity
    rows_x, rows_y, rows_z = velocity.shape
    station_count = station_cells.shape[0]
    offset_x = lax.axis_index("space") * rows_x
    grid_x = (lax.broadcasted_iota(jnp.int32, (rows_x, rows_y, rows_z), 0) + offset_x)[None]
    grid_y = lax.broadcasted_iota(jnp.int32, (rows_x, rows_y, rows_z), 1)[None]
    grid_z = lax.broadcasted_iota(jnp.int32, (rows_x, rows_y, rows_z), 2)[None]
    station_x = station_cells[:, 0][:, None, None, None]
    station_y = station_cells[:, 1][:, None, None, None]
    station_z = station_cells[:, 2][:, None, None, None]
    diff_x = (grid_x - station_x).astype(jnp.float32)
    diff_y = (grid_y - station_y).astype(jnp.float32)
    diff_z = (grid_z - station_z).astype(jnp.float32)
    times = jnp.sqrt(diff_x * diff_x + diff_y * diff_y + diff_z * diff_z)
    station_mask = (grid_x == station_x) & (grid_y == station_y) & (grid_z == station_z)
    for round_index in range(ROUNDS):
        tile_mask = (active[round_index][:, 0, :] > 0)[:, None, :, None, None]
        for sweep in range(SWEEPS):
            times = sweep_once(times, slowness, tile_mask, station_mask)
    cell_count = rows_x * rows_y * rows_z
    event_x = event_cells[0]
    event_y = event_cells[1]
    event_z = event_cells[2]
    local_x = event_x - offset_x
    inside = (local_x >= 0) & (local_x < rows_x)
    flat_index = jnp.where(
        inside, local_x * (rows_y * rows_z) + event_y * rows_z + event_z, cell_count
    )
    flat_times = times.reshape(station_count, cell_count)
    picked = jnp.take(flat_times, jnp.minimum(flat_index, cell_count - 1), axis=1)
    event_dx = (event_x[None, :] - station_cells[:, 0:1]).astype(jnp.float32)
    event_dy = (event_y[None, :] - station_cells[:, 1:2]).astype(jnp.float32)
    event_dz = (event_z[None, :] - station_cells[:, 2:3]).astype(jnp.float32)
    direct = jnp.sqrt(event_dx * event_dx + event_dy * event_dy + event_dz * event_dz)
    misfit = jnp.where(inside[None, :], picked - direct - delays, 0.0)
    source = (
        jnp.zeros((station_count, cell_count), jnp.float32)
        .at[:, flat_index]
        .add(misfit, mode="drop")
    )
    source = source.reshape(times.shape)
    final_ext = padded(times, (("space", 1),), 1)
    low_rim, high_rim = outer_rims(final_ext)
    time_around = six_neighbours(times, low_rim, high_rim, BIG)
    weights = [
        jnp.maximum(neighbour - times, 0.0) * velocity[None] / 6.0 for neighbour in time_around
    ]
    adjoint = source
    for sweep in range(ADJ_SWEEPS):
        adjoint_ext = padded(adjoint, (("space", 1),), 1)
        adjoint_around = six_neighbours(adjoint, adjoint_ext[:, :1], adjoint_ext[:, -1:], 0.0)
        summed = source
        for weight, neighbour in zip(weights, adjoint_around):
            summed = summed + weight * neighbour
        adjoint = summed
    density = slowness * jnp.sum(adjoint, axis=0)
    summed_density = lax.psum(density, "src")
    extended = padded(summed_density, (("space", 0),), 1)
    along_x = smooth_along(extended, 0)
    along_y = smooth_along(pad_zero(along_x, 1), 1)
    filtered = smooth_along(pad_zero(along_y, 2), 2)
    row_count = rows_y // lax.axis_size("src")
    kernel = lax.dynamic_slice_in_dim(filtered, lax.axis_index("src") * row_count, row_count, 1)
    return (times, kernel)


def solution(mesh):
    return jax.shard_map(
        per_device,
        mesh=mesh,
        in_specs=(
            P("space", None, None),
            P("src", None),
            P(),
            P("src", None),
            P(None, "src", "space", None),
        ),
        out_specs=(P("src", "space", None, None), P("space", "src", None)),
        check_vma=False,
    )
```

profile of v0, /device:TPU:7, one launch (start us, length us, event | category | flops | bytes accessed | tf_op | source)
XLA Modules:
  0.0 427.6 jit_solution(12294616544357058122)
XLA Ops:
  7.2 0.6 copy-done.5
  7.9 0.6 fusion.56
  9.1 1.3 add_sqrt_fusion
  10.4 2.6 collective-permute-start.1
  13.0 3.9 collective-permute-start
  17.5 0.6 multiply_add_fusion.3
  18.1 0.7 copy-done.6
  19.4 0.2 fusion.55
  19.7 2.1 collective-permute-done.1
  21.8 3.2 collective-permute-done
  25.1 2.6 fusion.1
  27.6 11.2 %collective-permute-start.3 = (f32[1,1,512,256]{3,2,1,0:T(8,128)S(1)}, f32[1,1,512,256]{3,2,1,0:T(8,128)S(1)}, u32[]{:S(2)}, u32[]{:S(2)}) collective-permute-start(f32[1,1,512,256]{3,2,1,0:T(8,128)S(1)} %fusion.1), channel_id=1, source_target_pairs={{1,0},{2,1},{3,2},{4,3},{5,4},{6,5},{7,6},{8,7},{9,8},{10,9},{11,1... | collective-permute-start | bytes 1572872 | tf_op jit(solution)/shard_map/ppermute | solution.py:23
  38.9 1.9 collective-permute-start.2
  40.8 0.2 fusion.53
  41.1 5.8 %collective-permute-done.2 = f32[1,1,512,256]{3,2,1,0:T(8,128)S(1)} collective-permute-done((f32[1,1,512,256]{3,2,1,0:T(8,128)S(1)}, f32[1,1,512,256]{3,2,1,0:T(8,128)S(1)}, u32[]{:S(2)}, u32[]{:S(2)}) %collective-permute-start.2) | collective-permute-done | bytes 524320 | tf_op jit(solution)/shard_map/ppermute | solution.py:22
  46.9 2.3 fusion.3
  49.2 6.5 %collective-permute-start.5 = (f32[1,1,512,256]{3,2,1,0:T(8,128)S(1)}, f32[1,1,512,256]{3,2,1,0:T(8,128)S(1)}, u32[]{:S(2)}, u32[]{:S(2)}) collective-permute-start(f32[1,1,512,256]{3,2,1,0:T(8,128)S(1)} %fusion.3), channel_id=1, source_target_pairs={{1,0},{2,1},{3,2},{4,3},{5,4},{6,5},{7,6},{8,7},{9,8},{10,9},{11,1... | collective-permute-start | bytes 1572872 | tf_op jit(solution)/shard_map/ppermute | solution.py:23
  55.7 1.9 collective-permute-start.4
  57.9 2.5 collective-permute-done.5
  60.4 3.3 collective-permute-done.4
  63.7 2.3 fusion.5
  66.0 6.5 %collective-permute-start.7 = (f32[1,1,512,256]{3,2,1,0:T(8,128)S(1)}, f32[1,1,512,256]{3,2,1,0:T(8,128)S(1)}, u32[]{:S(2)}, u32[]{:S(2)}) collective-permute-start(f32[1,1,512,256]{3,2,1,0:T(8,128)S(1)} %fusion.5), channel_id=1, source_target_pairs={{1,0},{2,1},{3,2},{4,3},{5,4},{6,5},{7,6},{8,7},{9,8},{10,9},{11,1... | collective-permute-start | bytes 1572872 | tf_op jit(solution)/shard_map/ppermute | solution.py:23
  72.5 1.9 collective-permute-start.6
  74.4 0.2 fusion.49
  74.7 2.5 collective-permute-done.7
  77.2 3.3 collective-permute-done.6
  80.5 2.3 fusion.7
  82.8 0.3 copy.7
  83.1 45.5 %gather_fusion = f32[8192]{0:T(1024)S(1)} fusion(f32[131072]{0:T(1024)S(1)} %bitcast.79, s32[8192]{0:T(1024)S(1)} %broadcast_clamp_fusion), kind=kCustom, calls=%fused_computation | custom fusion | bytes 98304 | tf_op jit(solution)/shard_map/jit(_take)/gather | solution.py:152
  128.6 2.1 subtract_select_fusion
  130.7 43.3 %scatter_custom_fusion = f32[131072]{0:T(1024)S(1)} fusion(s32[8192]{0:T(1024)S(1)} %bitcast.84, f32[8192]{0:T(1024)S(1)} %bitcast.83, f32[]{:T(128)} %constant.24.clone.1), kind=kCustom, calls=%fused_computation.66 | custom fusion | flops 8192 | bytes 524292 | tf_op jit(solution)/shard_map/scatter-add | solution.py:161
  174.2 6.5 %collective-permute-start.11 = (f32[1,1,512,256]{3,2,1,0:T(8,128)S(1)}, f32[1,1,512,256]{3,2,1,0:T(8,128)S(1)}, u32[]{:S(2)}, u32[]{:S(2)}) collective-permute-start(f32[1,1,512,256]{3,2,1,0:T(8,128)S(1)} %reshape.397), channel_id=1, source_target_pairs={{1,0},{2,1},{3,2},{4,3},{5,4},{6,5},{7,6},{8,7},{9,8},{10,9},{11,1... | collective-permute-start | bytes 1572872 | tf_op jit(solution)/shard_map/ppermute | solution.py:23
  180.7 1.9 collective-permute-start.9
  182.6 2.4 collective-permute-start.10
  185.1 3.3 collective-permute-start.8
  188.4 0.4 fusion.44
  189.0 4.2 collective-permute-done.10
  193.1 1.2 collective-permute-done.8
  194.4 0.9 multiply_add_fusion.2
  195.3 8.6 %collective-permute-start.13 = (f32[1,1,512,256]{3,2,1,0:T(8,128)S(1)}, f32[1,1,512,256]{3,2,1,0:T(8,128)S(1)}, u32[]{:S(2)}, u32[]{:S(2)}) collective-permute-start(f32[1,1,512,256]{3,2,1,0:T(8,128)S(1)} %get-tuple-element.4), channel_id=1, source_target_pairs={{1,0},{2,1},{3,2},{4,3},{5,4},{6,5},{7,6},{8,7},{9,8},{10,9},{11,1... | collective-permute-start | bytes 1572872 | tf_op jit(solution)/shard_map/ppermute | solution.py:23
  203.8 1.9 collective-permute-start.12
  205.8 0.2 fusion.43
  206.1 0.5 collective-permute-done.13
  206.5 5.4 %collective-permute-done.12 = f32[1,1,512,256]{3,2,1,0:T(8,128)S(1)} collective-permute-done((f32[1,1,512,256]{3,2,1,0:T(8,128)S(1)}, f32[1,1,512,256]{3,2,1,0:T(8,128)S(1)}, u32[]{:S(2)}, u32[]{:S(2)}) %collective-permute-start.12) | collective-permute-done | bytes 524320 | tf_op jit(solution)/shard_map/ppermute | solution.py:22
  211.9 0.5 multiply_add_fusion.1
  212.4 6.5 %collective-permute-start.15 = (f32[1,1,512,256]{3,2,1,0:T(8,128)S(1)}, f32[1,1,512,256]{3,2,1,0:T(8,128)S(1)}, u32[]{:S(2)}, u32[]{:S(2)}) collective-permute-start(f32[1,1,512,256]{3,2,1,0:T(8,128)S(1)} %multiply_add_fusion.1), channel_id=1, source_target_pairs={{1,0},{2,1},{3,2},{4,3},{5,4},{6,5},{7,6},{8,7},{9,8},{10,9},{11,1... | collective-permute-start | bytes 1572872 | tf_op jit(solution)/shard_map/ppermute | solution.py:23
  218.9 1.9 collective-permute-start.14
  220.8 0.2 fusion.41
  221.1 2.5 collective-permute-done.15
  223.6 3.3 collective-permute-done.14
  226.9 0.5 multiply_add_fusion
  227.4 6.5 %collective-permute-start.17 = (f32[1,1,512,256]{3,2,1,0:T(8,128)S(1)}, f32[1,1,512,256]{3,2,1,0:T(8,128)S(1)}, u32[]{:S(2)}, u32[]{:S(2)}) collective-permute-start(f32[1,1,512,256]{3,2,1,0:T(8,128)S(1)} %multiply_add_fusion), channel_id=1, source_target_pairs={{1,0},{2,1},{3,2},{4,3},{5,4},{6,5},{7,6},{8,7},{9,8},{10,9},{11,1... | collective-permute-start | bytes 1572872 | tf_op jit(solution)/shard_map/ppermute | solution.py:23
  233.9 1.9 collective-permute-start.16
  236.1 2.5 collective-permute-done.17
  238.6 3.3 collective-permute-done.16
  241.9 1.4 bitcast_multiply_fusion
  243.3 152.4 %all-reduce.40.cloned.1.call-done = f32[1,512,256]{2,1,0:T(8,128)} async-done(((f32[1,512,256]{2,1,0:T(8,128)}), f32[1,512,256]{2,1,0:T(8,128)}) %all-reduce.40.cloned.1.call-update) | async-done | bytes 524304 | tf_op jit(solution)/shard_map/psum | solution.py:179
  395.8 13.0 %collective-permute-start.19 = (f32[1,512,256]{2,1,0:T(8,128)}, f32[1,512,256]{2,1,0:T(8,128)S(1)}, u32[]{:S(2)}, u32[]{:S(2)}) collective-permute-start(f32[1,512,256]{2,1,0:T(8,128)} %all-reduce.40.cloned.1.call-done), channel_id=1, source_target_pairs={{1,0},{2,1},{3,2},{4,3},{5,4},{6,5},{7,6},{8,7},{9,8},{10,9},{11,1... | collective-permute-start | bytes 1572872 | tf_op jit(solution)/shard_map/ppermute | solution.py:23
  408.8 3.2 collective-permute-start.18
  412.0 5.4 %collective-permute-done.19 = f32[1,512,256]{2,1,0:T(8,128)S(1)} collective-permute-done((f32[1,512,256]{2,1,0:T(8,128)}, f32[1,512,256]{2,1,0:T(8,128)S(1)}, u32[]{:S(2)}, u32[]{:S(2)}) %collective-permute-start.19) | collective-permute-done | bytes 524320 | tf_op jit(solution)/shard_map/ppermute | solution.py:23
  417.4 1.0 collective-permute-done.18
  418.4 1.1 broadcast_multiply_fusion.1
  419.7 0.3 pad_slice_fusion.1
  420.1 0.6 fusion.31
  (38 shorter events, 2.2 us)
Async XLA Ops:
  7.2 388.6 %all-reduce.40.cloned.1.call-start = ((), (), s32[]{:S(2)}) async-start(), calls=%async_computation | async-start | bytes 1048576 | tf_op jit(solution)/shard_map/psum | solution.py:179
  7.2 0.7 copy-start.5
  9.1 10.1 %copy-start.3 = (s32[3,8192]{1,0:T(4,128)S(1)}, s32[3,8192]{1,0:T(4,128)}, u32[]{:S(2)}) copy-start(s32[3,8192]{1,0:T(4,128)} %param.7) | copy-start | bytes 294916
  10.4 11.4 %collective-permute-start.1 = (f32[1,1,512,256]{3,2,1,0:T(8,128)S(1)}, f32[1,1,512,256]{3,2,1,0:T(8,128)S(1)}, u32[]{:S(2)}, u32[]{:S(2)}) collective-permute-start(f32[1,1,512,256]{3,2,1,0:T(8,128)S(1)} %add_sqrt_fusion), channel_id=1, source_target_pairs={{1,0},{2,1},{3,2},{4,3},{5,4},{6,5},{7,6},{8,7},{9,8},{10,9},{11,1... | collective-permute-start | bytes 1572872 | tf_op jit(solution)/shard_map/ppermute | solution.py:23
  13.0 12.1 %collective-permute-start = (f32[1,1,512,256]{3,2,1,0:T(8,128)S(1)}, f32[1,1,512,256]{3,2,1,0:T(8,128)S(1)}, u32[]{:S(2)}, u32[]{:S(2)}) collective-permute-start(f32[1,1,512,256]{3,2,1,0:T(8,128)S(1)} %add_sqrt_fusion), channel_id=1, source_target_pairs={{0,1},{1,2},{2,3},{3,4},{4,5},{5,6},{6,7},{7,8},{8,9},{9,10},{10,1... | collective-permute-start | bytes 1572872 | tf_op jit(solution)/shard_map/ppermute | solution.py:22
  18.1 0.7 copy-start.6
  19.6 5.4 %copy-start.1 = (f32[1,512,256]{2,1,0:T(8,128)S(1)}, f32[1,512,256]{2,1,0:T(8,128)}, u32[]{:S(2)}) copy-start(f32[1,512,256]{2,1,0:T(8,128)} %param.5) | copy-start | bytes 1572868
  27.6 13.4 %collective-permute-start.3 = (f32[1,1,512,256]{3,2,1,0:T(8,128)S(1)}, f32[1,1,512,256]{3,2,1,0:T(8,128)S(1)}, u32[]{:S(2)}, u32[]{:S(2)}) collective-permute-start(f32[1,1,512,256]{3,2,1,0:T(8,128)S(1)} %fusion.1), channel_id=1, source_target_pairs={{1,0},{2,1},{3,2},{4,3},{5,4},{6,5},{7,6},{8,7},{9,8},{10,9},{11,1... | collective-permute-start | bytes 1572872 | tf_op jit(solution)/shard_map/ppermute | solution.py:23
  38.9 8.0 %collective-permute-start.2 = (f32[1,1,512,256]{3,2,1,0:T(8,128)S(1)}, f32[1,1,512,256]{3,2,1,0:T(8,128)S(1)}, u32[]{:S(2)}, u32[]{:S(2)}) collective-permute-start(f32[1,1,512,256]{3,2,1,0:T(8,128)S(1)} %fusion.1), channel_id=1, source_target_pairs={{0,1},{1,2},{2,3},{3,4},{4,5},{5,6},{6,7},{7,8},{8,9},{9,10},{10,1... | collective-permute-start | bytes 1572872 | tf_op jit(solution)/shard_map/ppermute | solution.py:22
  49.2 11.2 %collective-permute-start.5 = (f32[1,1,512,256]{3,2,1,0:T(8,128)S(1)}, f32[1,1,512,256]{3,2,1,0:T(8,128)S(1)}, u32[]{:S(2)}, u32[]{:S(2)}) collective-permute-start(f32[1,1,512,256]{3,2,1,0:T(8,128)S(1)} %fusion.3), channel_id=1, source_target_pairs={{1,0},{2,1},{3,2},{4,3},{5,4},{6,5},{7,6},{8,7},{9,8},{10,9},{11,1... | collective-permute-start | bytes 1572872 | tf_op jit(solution)/shard_map/ppermute | solution.py:23
  55.7 8.0 %collective-permute-start.4 = (f32[1,1,512,256]{3,2,1,0:T(8,128)S(1)}, f32[1,1,512,256]{3,2,1,0:T(8,128)S(1)}, u32[]{:S(2)}, u32[]{:S(2)}) collective-permute-start(f32[1,1,512,256]{3,2,1,0:T(8,128)S(1)} %fusion.3), channel_id=1, source_target_pairs={{0,1},{1,2},{2,3},{3,4},{4,5},{5,6},{6,7},{7,8},{8,9},{9,10},{10,1... | collective-permute-start | bytes 1572872 | tf_op jit(solution)/shard_map/ppermute | solution.py:22
  66.0 11.2 %collective-permute-start.7 = (f32[1,1,512,256]{3,2,1,0:T(8,128)S(1)}, f32[1,1,512,256]{3,2,1,0:T(8,128)S(1)}, u32[]{:S(2)}, u32[]{:S(2)}) collective-permute-start(f32[1,1,512,256]{3,2,1,0:T(8,128)S(1)} %fusion.5), channel_id=1, source_target_pairs={{1,0},{2,1},{3,2},{4,3},{5,4},{6,5},{7,6},{8,7},{9,8},{10,9},{11,1... | collective-permute-start | bytes 1572872 | tf_op jit(solution)/shard_map/ppermute | solution.py:23
  72.5 8.0 %collective-permute-start.6 = (f32[1,1,512,256]{3,2,1,0:T(8,128)S(1)}, f32[1,1,512,256]{3,2,1,0:T(8,128)S(1)}, u32[]{:S(2)}, u32[]{:S(2)}) collective-permute-start(f32[1,1,512,256]{3,2,1,0:T(8,128)S(1)} %fusion.5), channel_id=1, source_target_pairs={{0,1},{1,2},{2,3},{3,4},{4,5},{5,6},{6,7},{7,8},{8,9},{9,10},{10,1... | collective-permute-start | bytes 1572872 | tf_op jit(solution)/shard_map/ppermute | solution.py:22
  82.8 111.6 %copy-start = (f32[1,1,512,256]{3,2,1,0:T(8,128)}, f32[1,1,512,256]{3,2,1,0:T(8,128)S(1)}, u32[]{:S(2)}) copy-start(f32[1,1,512,256]{3,2,1,0:T(8,128)S(1)} %fusion.7) | copy-start | bytes 1572868
  83.1 45.6 %copy-start.4 = (f32[1,8192]{1,0:T(1,128)S(1)}, f32[1,8192]{1,0:T(1,128)}, u32[]{:S(2)}) copy-start(f32[1,8192]{1,0:T(1,128)} %param.8) | copy-start | bytes 98308
  174.2 14.7 %collective-permute-start.11 = (f32[1,1,512,256]{3,2,1,0:T(8,128)S(1)}, f32[1,1,512,256]{3,2,1,0:T(8,128)S(1)}, u32[]{:S(2)}, u32[]{:S(2)}) collective-permute-start(f32[1,1,512,256]{3,2,1,0:T(8,128)S(1)} %reshape.397), channel_id=1, source_target_pairs={{1,0},{2,1},{3,2},{4,3},{5,4},{6,5},{7,6},{8,7},{9,8},{10,9},{11,1... | collective-permute-start | bytes 1572872 | tf_op jit(solution)/shard_map/ppermute | solution.py:23
  180.7 8.2 %collective-permute-start.9 = (f32[1,1,512,256]{3,2,1,0:T(8,128)S(1)}, f32[1,1,512,256]{3,2,1,0:T(8,128)S(1)}, u32[]{:S(2)}, u32[]{:S(2)}) collective-permute-start(f32[1,1,512,256]{3,2,1,0:T(8,128)S(1)} %reshape.397), channel_id=1, source_target_pairs={{0,1},{1,2},{2,3},{3,4},{4,5},{5,6},{6,7},{7,8},{8,9},{9,10},{10,1... | collective-permute-start | bytes 1572872 | tf_op jit(solution)/shard_map/ppermute | solution.py:22
  182.6 10.5 %collective-permute-start.10 = (f32[1,1,512,256]{3,2,1,0:T(8,128)S(1)}, f32[1,1,512,256]{3,2,1,0:T(8,128)S(1)}, u32[]{:S(2)}, u32[]{:S(2)}) collective-permute-start(f32[1,1,512,256]{3,2,1,0:T(8,128)S(1)} %fusion.7), channel_id=1, source_target_pairs={{1,0},{2,1},{3,2},{4,3},{5,4},{6,5},{7,6},{8,7},{9,8},{10,9},{11,1... | collective-permute-start | bytes 1572872 | tf_op jit(solution)/shard_map/ppermute | solution.py:23
  185.1 9.3 %collective-permute-start.8 = (f32[1,1,512,256]{3,2,1,0:T(8,128)S(1)}, f32[1,1,512,256]{3,2,1,0:T(8,128)S(1)}, u32[]{:S(2)}, u32[]{:S(2)}) collective-permute-start(f32[1,1,512,256]{3,2,1,0:T(8,128)S(1)} %fusion.7), channel_id=1, source_target_pairs={{0,1},{1,2},{2,3},{3,4},{4,5},{5,6},{6,7},{7,8},{8,9},{9,10},{10,1... | collective-permute-start | bytes 1572872 | tf_op jit(solution)/shard_map/ppermute | solution.py:22
  195.3 11.2 %collective-permute-start.13 = (f32[1,1,512,256]{3,2,1,0:T(8,128)S(1)}, f32[1,1,512,256]{3,2,1,0:T(8,128)S(1)}, u32[]{:S(2)}, u32[]{:S(2)}) collective-permute-start(f32[1,1,512,256]{3,2,1,0:T(8,128)S(1)} %get-tuple-element.4), channel_id=1, source_target_pairs={{1,0},{2,1},{3,2},{4,3},{5,4},{6,5},{7,6},{8,7},{9,8},{10,9},{11,1... | collective-permute-start | bytes 1572872 | tf_op jit(solution)/shard_map/ppermute | solution.py:23
  203.8 8.0 %collective-permute-start.12 = (f32[1,1,512,256]{3,2,1,0:T(8,128)S(1)}, f32[1,1,512,256]{3,2,1,0:T(8,128)S(1)}, u32[]{:S(2)}, u32[]{:S(2)}) collective-permute-start(f32[1,1,512,256]{3,2,1,0:T(8,128)S(1)} %get-tuple-element.4), channel_id=1, source_target_pairs={{0,1},{1,2},{2,3},{3,4},{4,5},{5,6},{6,7},{7,8},{8,9},{9,10},{10,1... | collective-permute-start | bytes 1572872 | tf_op jit(solution)/shard_map/ppermute | solution.py:22
  212.4 11.2 %collective-permute-start.15 = (f32[1,1,512,256]{3,2,1,0:T(8,128)S(1)}, f32[1,1,512,256]{3,2,1,0:T(8,128)S(1)}, u32[]{:S(2)}, u32[]{:S(2)}) collective-permute-start(f32[1,1,512,256]{3,2,1,0:T(8,128)S(1)} %multiply_add_fusion.1), channel_id=1, source_target_pairs={{1,0},{2,1},{3,2},{4,3},{5,4},{6,5},{7,6},{8,7},{9,8},{10,9},{11,1... | collective-permute-start | bytes 1572872 | tf_op jit(solution)/shard_map/ppermute | solution.py:23
  218.9 8.0 %collective-permute-start.14 = (f32[1,1,512,256]{3,2,1,0:T(8,128)S(1)}, f32[1,1,512,256]{3,2,1,0:T(8,128)S(1)}, u32[]{:S(2)}, u32[]{:S(2)}) collective-permute-start(f32[1,1,512,256]{3,2,1,0:T(8,128)S(1)} %multiply_add_fusion.1), channel_id=1, source_target_pairs={{0,1},{1,2},{2,3},{3,4},{4,5},{5,6},{6,7},{7,8},{8,9},{9,10},{10,1... | collective-permute-start | bytes 1572872 | tf_op jit(solution)/shard_map/ppermute | solution.py:22
  227.4 11.2 %collective-permute-start.17 = (f32[1,1,512,256]{3,2,1,0:T(8,128)S(1)}, f32[1,1,512,256]{3,2,1,0:T(8,128)S(1)}, u32[]{:S(2)}, u32[]{:S(2)}) collective-permute-start(f32[1,1,512,256]{3,2,1,0:T(8,128)S(1)} %multiply_add_fusion), channel_id=1, source_target_pairs={{1,0},{2,1},{3,2},{4,3},{5,4},{6,5},{7,6},{8,7},{9,8},{10,9},{11,1... | collective-permute-start | bytes 1572872 | tf_op jit(solution)/shard_map/ppermute | solution.py:23
  233.9 8.0 %collective-permute-start.16 = (f32[1,1,512,256]{3,2,1,0:T(8,128)S(1)}, f32[1,1,512,256]{3,2,1,0:T(8,128)S(1)}, u32[]{:S(2)}, u32[]{:S(2)}) collective-permute-start(f32[1,1,512,256]{3,2,1,0:T(8,128)S(1)} %multiply_add_fusion), channel_id=1, source_target_pairs={{0,1},{1,2},{2,3},{3,4},{4,5},{5,6},{6,7},{7,8},{8,9},{9,10},{10,1... | collective-permute-start | bytes 1572872 | tf_op jit(solution)/shard_map/ppermute | solution.py:22
  395.8 21.6 %collective-permute-start.19 = (f32[1,512,256]{2,1,0:T(8,128)}, f32[1,512,256]{2,1,0:T(8,128)S(1)}, u32[]{:S(2)}, u32[]{:S(2)}) collective-permute-start(f32[1,512,256]{2,1,0:T(8,128)} %all-reduce.40.cloned.1.call-done), channel_id=1, source_target_pairs={{1,0},{2,1},{3,2},{4,3},{5,4},{6,5},{7,6},{8,7},{9,8},{10,9},{11,1... | collective-permute-start | bytes 1572872 | tf_op jit(solution)/shard_map/ppermute | solution.py:23
  408.8 9.6 %collective-permute-start.18 = (f32[1,512,256]{2,1,0:T(8,128)}, f32[1,512,256]{2,1,0:T(8,128)S(1)}, u32[]{:S(2)}, u32[]{:S(2)}) collective-permute-start(f32[1,512,256]{2,1,0:T(8,128)} %all-reduce.40.cloned.1.call-done), channel_id=1, source_target_pairs={{0,1},{1,2},{2,3},{3,4},{4,5},{5,6},{6,7},{7,8},{8,9},{9,10},{10,1... | collective-permute-start | bytes 1572872 | tf_op jit(solution)/shard_map/ppermute | solution.py:22
  412.0 7.6 %copy-start.2 = (f32[1,512,256]{2,1,0:T(8,128)S(1)}, f32[1,512,256]{2,1,0:T(8,128)}, u32[]{:S(2)}) copy-start(f32[1,512,256]{2,1,0:T(8,128)} %all-reduce.40.cloned.1.call-done) | copy-start | bytes 1572868
Sparse Core Ops, SparseCore 0:
  243.5 152.2 all-reduce.39
where the time goes:
time: 432 us; the launch traced here: 428 us
  waiting for transfers between devices  204 us (47%)
  starting transfers between devices  94.2 us (22%)
  other arithmetic  62.1 us (14%)
  local copies, waits for them, and re-layouts  51.1 us (12%)
  between operations  15.8 us (4%)
    psum x1, waiting for transfers between devices, per_device(): summed_density = lax.psum(density, 'src')  152 us
    ppermute x10, starting transfers between devices, padded(): after = lax.ppermute(first, axis, down)  70.3 us
    gather x1, local copies, waits for them, and re-layouts, per_device(): jnp.take(flat_times, jnp.minimum(flat_index, cell_count - 1), axis=1)  45.5 us
    scatter-add x1, other arithmetic, per_device(): source = jnp.zeros((station_count, cell_count), jnp.float32).at[:, flat_i...  43.3 us
    ppermute x10, waiting for transfers between devices, padded(): before = lax.ppermute(last, axis, up)  29.8 us
    ppermute x10, starting transfers between devices, padded(): before = lax.ppermute(last, axis, up)  23.8 us
    ppermute x10, waiting for transfers between devices, padded(): after = lax.ppermute(first, axis, down)  22.3 us
    select_n x4, other arithmetic, sweep_once(): return jnp.where(station_mask, 0.0, chosen)  9.37 us
  transfers between devices with their start and end apart: 21, of which 18 were waited for; matrix products, arithmetic and copies ran while one was open for 1% of the time, Pallas kernels for 0%

commit v1 on v0

v1 whole, which is shorter than its diff:
```python
import functools

import jax
import jax.numpy as jnp
from jax import lax
from jax.experimental import pallas as pl
from jax.experimental.pallas import tpu as pltpu
from jax.sharding import PartitionSpec as P

TY = 32
BIG = 1000000.0
HALO = 8
GROUP = 2
MESH = pl.DeviceIdType.MESH


def godunov(near_x, near_y, near_z, cost):
    low_xy = jnp.minimum(near_x, near_y)
    high_xy = jnp.maximum(near_x, near_y)
    lowest = jnp.minimum(low_xy, near_z)
    rest = jnp.maximum(low_xy, near_z)
    middle = jnp.minimum(high_xy, rest)
    highest = jnp.maximum(high_xy, rest)
    gap2 = middle - lowest
    gap3 = highest - lowest
    cost_sq = cost * cost
    gap2_sq = gap2 * gap2
    disc2 = 2.0 * cost_sq - gap2_sq
    reach = gap3 + gap3 - gap2
    two = disc2 <= reach * reach
    step = gap3 - gap2
    disc3 = 3.0 * cost_sq - (gap2_sq + gap3 * gap3 + step * step)
    disc = jnp.where(two, disc2, disc3)
    base = jnp.where(two, gap2, gap2 + gap3)
    scale = jnp.where(two, 0.5, 1.0 / 3.0)
    wide = lowest + (base + jnp.sqrt(jnp.maximum(disc, 0.0))) * scale
    return jnp.where(cost <= gap2, lowest + cost, wide)


def beside(field, axis):
    length = field.shape[axis]
    return pltpu.roll(field, 1, axis), pltpu.roll(field, length - 1, axis)


def kernel(
    dims,
    velocity_ref,
    meta_ref,
    events_ref,
    delays_ref,
    times_out,
    kernel_out,
    vel,
    slow,
    meta,
    delay,
    start,
    time_a,
    time_b,
    count,
    late,
    masks,
    spot,
    weights,
    adj_a,
    adj_b,
    dens,
    part,
    parts,
    total,
    send_sem,
    recv_sem,
    last_sem,
):
    n_src, n_space, ny, nz, events = dims
    group = GROUP
    rows = ny // (n_space * group)
    peers = n_src // group
    chunk_x = n_space // peers
    own_rows = ny // n_src
    per_owner = own_rows // rows
    tall = rows + 2 * HALO
    s, p = lax.axis_index("src"), lax.axis_index("space")
    m, g = s // group, s % group
    block = g * n_space + p
    y_base = block * rows
    n_blocks = n_space * group

    def where_is(b):
        return (m * group + b // n_space, b % n_space)

    owner = block // per_owner
    targets = [(owner, chunk_x * m + k) for k in range(chunk_x)]
    sources = []
    for k in range(per_owner):
        b = s * per_owner + k
        sources.append(((p // chunk_x) * group + b // n_space, b % n_space))

    barrier = pltpu.get_barrier_semaphore()
    signals = 0
    for dg in range(group):
        for i in range(n_space):
            if dg or i:
                to = (m * group + (g + dg) % group, (p + i) % n_space)
                pl.semaphore_signal(barrier, inc=1, device_id=to, device_id_type=MESH)
                signals += 1
    for i in range(1, peers):
        to = (((m + i) % peers) * group + g, p)
        pl.semaphore_signal(barrier, inc=1, device_id=to, device_id_type=MESH)
        signals += 1
    for to in sources:
        mine = (to[0] == s) & (to[1] == p)

        @pl.when(jnp.logical_not(mine))
        def _():
            pl.semaphore_signal(barrier, inc=1, device_id=to, device_id_type=MESH)

        signals = signals + jnp.where(mine, 0, 1)
    pl.semaphore_wait(barrier, signals)

    own = pl.ds(HALO, rows)
    for i in range(n_space):
        q = (p + i) % n_space
        piece = velocity_ref.at[pl.ds(pl.multiple_of((g * n_space + q) * rows, 8), rows), :]
        if i == 0:
            pltpu.make_async_copy(piece, vel.at[own, p, :], recv_sem.at[0]).start()
        else:
            pltpu.make_async_remote_copy(
                piece,
                vel.at[own, p, :],
                send_sem.at[0],
                recv_sem.at[0],
                device_id=(s, q),
                device_id_type=MESH,
            ).start()
    for dg in range(group):
        for i in range(n_space):
            line = meta.at[g, pl.ds(p, 1), :]
            if dg == 0 and i == 0:
                pltpu.make_async_copy(meta_ref, line, recv_sem.at[1]).start()
            else:
                to = (m * group + (g + dg) % group, (p + i) % n_space)
                pltpu.make_async_remote_copy(
                    meta_ref,
                    line,
                    send_sem.at[1],
                    recv_sem.at[1],
                    device_id=to,
                    device_id_type=MESH,
                ).start()
    for dg in range(group):
        if dg == 0:
            pltpu.make_async_copy(delays_ref, delay.at[g], recv_sem.at[2]).start()
        else:
            pltpu.make_async_remote_copy(
                delays_ref,
                delay.at[g],
                send_sem.at[2],
                recv_sem.at[2],
                device_id=(m * group + (g + dg) % group, p),
                device_id_type=MESH,
            ).start()
    pltpu.make_async_copy(delay, delay, recv_sem.at[2]).wait()

    src_rows = rows + 10
    cells = src_rows * n_space
    step_events = 1024
    count[...] = jnp.zeros_like(count)
    late[...] = jnp.zeros_like(late)

    def add_events(c, carry):
        at = pl.ds(pl.multiple_of(c * step_events, step_events), step_events)
        event_x = events_ref[0:1, at]
        event_y = events_ref[1:2, at]
        event_z = events_ref[2:3, at]
        key = (event_y - (y_base - 5)) * n_space + event_x
        cell = lax.broadcasted_iota(jnp.int32, (cells, step_events), 0)
        left = jnp.where(cell == key, 1.0, 0.0).astype(jnp.bfloat16)
        deep = lax.broadcasted_iota(jnp.int32, (nz, step_events), 0) == event_z
        contract = (((1,), (1,)), ((), ()))

        def product(value):
            right = jnp.where(deep, value, 0.0).astype(jnp.bfloat16)
            return lax.dot_general(left, right, contract, preferred_element_type=jnp.float32)

        count[...] += product(1.0)
        for k in range(group):
            lateness = delay[k, 0:1, at]
            coarse = lateness.astype(jnp.bfloat16).astype(jnp.float32)
            late[k] += product(coarse) + product(lateness - coarse)
        return carry

    lax.fori_loop(0, events // step_events, add_events, 0)

    pltpu.make_async_copy(meta, meta, recv_sem.at[1]).wait()
    lane = lax.broadcasted_iota(jnp.int32, (n_space, 128), 1)
    layer = lax.broadcasted_iota(jnp.int32, (n_space, nz), 0)
    depth = lax.broadcasted_iota(jnp.int32, (n_space, nz), 1)
    layer_f = layer.astype(jnp.float32)
    depth_f = depth.astype(jnp.float32)
    first_tile = (y_base - HALO + TY) // TY - 1
    tiles = ny // TY

    def column(k, index):
        picked = jnp.where(lane == index, meta[k], 0.0)
        return jnp.broadcast_to(jnp.sum(picked, axis=1, keepdims=True), (n_space, nz))

    def row_valid(y):
        return (y >= 0) & (y < ny)

    for k in range(group):
        for r in range(2):
            for t in range(2):
                masks[r, k, t] = column(k, r * tiles + first_tile + t)
            masks[r, k, 2] = jnp.zeros((n_space, nz), jnp.float32)
        cell_x, cell_y, cell_z = column(k, 64), column(k, 65), column(k, 66)
        here = (layer_f == cell_x) & (depth_f == cell_z)
        spot[k] = jnp.where(here, cell_y, -1.0)
        flat = (layer_f - cell_x) * (layer_f - cell_x) + (depth_f - cell_z) * (depth_f - cell_z)

        def init_row(j, carry):
            y = y_base - HALO - 1 + j
            diff = y.astype(jnp.float32) - cell_y
            start[k, j] = jnp.where(row_valid(y), jnp.sqrt(flat + diff * diff), BIG)
            return carry

        lax.fori_loop(0, tall + 2, init_row, 0)
        time_a[k, 0] = start[k, 0]

    pltpu.make_async_copy(vel.at[own], vel.at[own], recv_sem.at[0]).wait()
    before = where_is((block + n_blocks - 1) % n_blocks)
    after = where_is((block + 1) % n_blocks)
    to_before = pltpu.make_async_remote_copy(
        vel.at[pl.ds(HALO, HALO)],
        vel.at[pl.ds(HALO + rows, HALO)],
        send_sem.at[3],
        recv_sem.at[3],
        device_id=before,
        device_id_type=MESH,
    )
    to_after = pltpu.make_async_remote_copy(
        vel.at[pl.ds(rows, HALO)],
        vel.at[pl.ds(0, HALO)],
        send_sem.at[4],
        recv_sem.at[4],
        device_id=after,
        device_id_type=MESH,
    )
    to_before.start()
    to_after.start()
    to_before.wait_recv()
    to_after.wait_recv()

    def slow_row(j, carry):
        slow[j] = 1.0 / vel[j]
        return carry

    lax.fori_loop(0, tall, slow_row, 0)

    def sweep(k, source, target, low, high, r):
        def row(j, carry):
            y = y_base - HALO + j
            centre = source[k, j + 1]
            near_y = jnp.minimum(source[k, j], source[k, j + 2])
            x_low, x_high = beside(centre, 0)
            x_low = jnp.where(layer == 0, BIG, x_low)
            x_high = jnp.where(layer == n_space - 1, BIG, x_high)
            z_low, z_high = beside(centre, 1)
            z_low = jnp.where(depth == 0, BIG, z_low)
            z_high = jnp.where(depth == nz - 1, BIG, z_high)
            update = godunov(
                jnp.minimum(x_low, x_high), near_y, jnp.minimum(z_low, z_high), slow[j]
            )
            kind = jnp.where(row_valid(y), (y + TY) // TY - 1 - first_tile, 2)
            chosen = (masks[r, k, kind] > 0.0) & (spot[k] != y.astype(jnp.float32))
            target[k, j + 1] = jnp.where(chosen, update, centre)
            return carry

        lax.fori_loop(low, high, row, 0)

    inner = pl.ds(HALO + 1, rows)
    for k in range(group):
        sweep(k, start, time_a, 0, tall, 0)
        sweep(k, time_a, time_b, 1, tall - 1, 0)
        sweep(k, time_b, time_a, 2, tall - 2, 1)
        sweep(k, time_a, time_b, 3, tall - 3, 1)
        for i in range(n_space):
            q = (p + i) % n_space
            piece = time_b.at[k, inner, q, :]
            place = times_out.at[pl.ds(pl.multiple_of(y_base, 8), rows), :]
            to_src = m * group + k

            def send(piece=piece, place=place, to_src=to_src, q=q):
                pltpu.make_async_remote_copy(
                    piece,
                    place,
                    send_sem.at[5],
                    recv_sem.at[5],
                    device_id=(to_src, q),
                    device_id_type=MESH,
                ).start()

            if i:
                send()
            else:

                @pl.when(g == k)
                def _():
                    pltpu.make_async_copy(piece, place, recv_sem.at[5]).start()

                @pl.when(g != k)
                def _():
                    send()

    dens[...] = jnp.zeros_like(dens)
    for k in range(group):

        def source_row(i, carry):
            j = i + 3
            at = pl.ds(pl.multiple_of(i * n_space, n_space), n_space)
            value = count[at, :] * (time_b[k, j + 1] - start[k, j + 1]) - late[k, at, :]
            adj_a[0, i] = value
            adj_a[1, i] = value
            return carry

        lax.fori_loop(0, src_rows, source_row, 0)

        def weight_row(i, carry):
            j = i + 4
            centre = time_b[k, j + 1]
            rate = vel[j] * (1.0 / 6.0)
            x_low, x_high = beside(centre, 0)
            z_low, z_high = beside(centre, 1)
            around = (
                jnp.where(layer == 0, centre, x_low),
                jnp.where(layer == n_space - 1, centre, x_high),
                time_b[k, j],
                time_b[k, j + 2],
                jnp.where(depth == 0, centre, z_low),
                jnp.where(depth == nz - 1, centre, z_high),
            )
            for d, near in enumerate(around):
                weights[d, i] = jnp.maximum(near - centre, 0.0) * rate
            return carry

        lax.fori_loop(0, src_rows - 2, weight_row, 0)

        def adjoint_sweep(old, new, low, high):
            def row(i, carry):
                centre = old[i]
                x_low, x_high = beside(centre, 0)
                z_low, z_high = beside(centre, 1)
                value = adj_a[0, i]
                around = (x_low, x_high, old[i - 1], old[i + 1], z_low, z_high)
                for d, near in enumerate(around):
                    value = value + weights[d, i - 1] * near
                new[i] = value
                return carry

            lax.fori_loop(low, high, row, 0)

        adjoint_sweep(adj_a.at[1], adj_b, 1, src_rows - 1)
        adjoint_sweep(adj_b, adj_a.at[1], 2, src_rows - 2)
        adjoint_sweep(adj_a.at[1], adj_b, 3, src_rows - 3)
        adjoint_sweep(adj_b, adj_a.at[1], 4, src_rows - 4)

        def density_row(i, carry):
            dens[i] += slow[i + HALO - 1] * adj_a[1, i + 4]
            return carry

        lax.fori_loop(0, rows + 2, density_row, 0)

    def smooth_row(i, carry):
        value = dens[i] + 2.0 * dens[i + 1] + dens[i + 2]
        x_low, x_high = beside(value, 0)
        x_low = jnp.where(layer == 0, 0.0, x_low)
        x_high = jnp.where(layer == n_space - 1, 0.0, x_high)
        value = x_low + 2.0 * value + x_high
        z_low, z_high = beside(value, 1)
        z_low = jnp.where(depth == 0, 0.0, z_low)
        z_high = jnp.where(depth == nz - 1, 0.0, z_high)
        part[i] = (z_low + 2.0 * value + z_high) * (1.0 / 64.0)
        return carry

    lax.fori_loop(0, rows, smooth_row, 0)

    for i in range(peers):
        q = (m + i) % peers
        piece = part.at[:, pl.ds(pl.multiple_of(q * chunk_x, chunk_x), chunk_x), :]
        if i == 0:
            pltpu.make_async_copy(piece, parts.at[m], recv_sem.at[6]).start()
        else:
            pltpu.make_async_remote_copy(
                piece,
                parts.at[m],
                send_sem.at[6],
                recv_sem.at[6],
                device_id=(q * group + g, p),
                device_id_type=MESH,
            ).start()
    pltpu.make_async_copy(parts, parts, recv_sem.at[6]).wait()
    summed = parts[0]
    for i in range(1, peers):
        summed = summed + parts[i]
    total[...] = summed
    place_k = block % per_owner
    for k in range(chunk_x):
        to = targets[k]
        piece = total.at[:, k, :]
        place = kernel_out.at[pl.ds(pl.multiple_of(place_k * rows, 8), rows), :]
        mine = (to[0] == s) & (to[1] == p)

        @pl.when(mine)
        def _():
            pltpu.make_async_copy(piece, place, recv_sem.at[7]).start()

        @pl.when(jnp.logical_not(mine))
        def _():
            pltpu.make_async_remote_copy(
                piece,
                place,
                last_sem.at[k],
                recv_sem.at[7],
                device_id=to,
                device_id_type=MESH,
            ).start()

    def drain(ref, sem):
        pltpu.make_async_copy(ref, ref, sem).wait()

    for k in range(chunk_x):
        to = targets[k]
        mine = (to[0] == s) & (to[1] == p)

        @pl.when(jnp.logical_not(mine))
        def _():
            drain(total.at[:, k, :], last_sem.at[k])

    drain(velocity_ref.at[pl.ds(0, (n_space - 1) * rows), :], send_sem.at[0])
    for k in range(group):
        if k:
            drain(meta.at[k], send_sem.at[1])
        else:
            drain(meta.at[k, pl.ds(0, n_space - 8), :], send_sem.at[1])
            for _ in range(7):
                drain(meta_ref, send_sem.at[1])
    if group > 1:
        drain(delay.at[pl.ds(1, group - 1)], send_sem.at[2])
    to_before.wait_send()
    to_after.wait_send()
    drain(times_out.at[pl.ds(0, (n_blocks - 1) * rows), :], send_sem.at[5])
    drain(parts.at[pl.ds(1, peers - 1)], send_sem.at[6])
    drain(times_out, recv_sem.at[5])
    drain(kernel_out, recv_sem.at[7])


def per_device(dims, velocity, station_cells, event_cells, delays, active):
    n_src, n_space, ny, nz, events = dims
    rows = ny // (n_space * GROUP)
    tall = rows + 2 * HALO
    peers = n_src // GROUP
    chunk_x = n_space // peers
    own_rows = ny // n_src
    src_rows = rows + 10
    flags = active.reshape(1, -1).astype(jnp.float32)
    cells = station_cells.astype(jnp.float32)
    meta = jnp.concatenate(
        [
            flags,
            jnp.zeros((1, 64 - flags.shape[1]), jnp.float32),
            cells,
            jnp.zeros((1, 61), jnp.float32),
        ],
        axis=1,
    )
    f32 = jnp.float32
    plane = (n_space, nz)
    vmem = pl.BlockSpec(memory_space=pltpu.VMEM)
    anywhere = pl.BlockSpec(memory_space=pl.ANY)
    times, kernel_part = pl.pallas_call(
        functools.partial(kernel, dims),
        out_shape=(
            jax.ShapeDtypeStruct((ny, nz), f32),
            jax.ShapeDtypeStruct((own_rows, nz), f32),
        ),
        in_specs=[anywhere, vmem, vmem, vmem],
        out_specs=(anywhere, anywhere),
        scratch_shapes=[
            pltpu.VMEM((tall,) + plane, f32),
            pltpu.VMEM((tall,) + plane, f32),
            pltpu.VMEM((GROUP, n_space, 128), f32),
            pltpu.VMEM((GROUP, 1, events), f32),
            pltpu.VMEM((GROUP, tall + 2) + plane, f32),
            pltpu.VMEM((GROUP, tall + 2) + plane, f32),
            pltpu.VMEM((GROUP, tall + 2) + plane, f32),
            pltpu.VMEM((src_rows * n_space, nz), f32),
            pltpu.VMEM((GROUP, src_rows * n_space, nz), f32),
            pltpu.VMEM((2, GROUP, 3) + plane, f32),
            pltpu.VMEM((GROUP,) + plane, f32),
            pltpu.VMEM((6, src_rows - 2) + plane, f32),
            pltpu.VMEM((2, src_rows) + plane, f32),
            pltpu.VMEM((src_rows,) + plane, f32),
            pltpu.VMEM((rows + 2,) + plane, f32),
            pltpu.VMEM((rows,) + plane, f32),
            pltpu.VMEM((peers, rows, chunk_x, nz), f32),
            pltpu.VMEM((rows, chunk_x, nz), f32),
            pltpu.SemaphoreType.DMA((8,)),
            pltpu.SemaphoreType.DMA((8,)),
            pltpu.SemaphoreType.DMA((chunk_x,)),
        ],
        compiler_params=pltpu.CompilerParams(
            collective_id=0, has_side_effects=True, vmem_limit_bytes=48 << 20
        ),
    )(velocity[0], meta, event_cells, delays)
    return times[None, None], kernel_part[None]


def solution(mesh):
    n_src, n_space = mesh.shape["src"], mesh.shape["space"]

    def run(velocity, station_cells, event_cells, delays, active):
        dims = (n_src, n_space, velocity.shape[1], velocity.shape[2], event_cells.shape[1])
        return jax.shard_map(
            functools.partial(per_device, dims),
            mesh=mesh,
            in_specs=(
                P("space", None, None),
                P("src", None),
                P(),
                P("src", None),
                P(None, "src", "space", None),
            ),
            out_specs=(P("src", "space", None, None), P("space", "src", None)),
            check_vma=False,
        )(velocity, station_cells, event_cells, delays, active)

    return run
```

time: 432 us -> 101 us (0.23)
  waiting for transfers between devices: 204 us -> 0 us
  starting transfers between devices: 94.2 us -> 0 us
  Pallas kernels: 0 us -> 93.7 us
  other arithmetic: 62.1 us -> 0.1 us
  local copies, waits for them, and re-layouts: 51.1 us -> 5.52 us
  between operations: 15.8 us -> 0.65 us
    psum x1 -> x0, waiting for transfers between devices: 152 us -> none  [per_device(): summed_density = lax.psum(density, 'src')]
    ppermute x20 -> x0, starting transfers between devices: 94.1 us -> none  [the longest x10 70.3 us: padded(): after = lax.ppermute(first, axis, down)]
    pallas_call x0 -> x1, Pallas kernels: none -> 93.7 us  [per_device(): pl.pallas_call(functools.partial(kernel, dims), out_shape=(jax.ShapeDtype...]
    ppermute x20 -> x0, waiting for transfers between devices: 52 us -> none  [the longest x10 29.8 us: padded(): before = lax.ppermute(last, axis, up)]
    gather x1 -> x0, local copies, waits for them, and re-layouts: 45.5 us -> none  [per_device(): jnp.take(flat_times, jnp.minimum(flat_index, cell_count - 1), axis=1)]
    scatter-add x1 -> x0, other arithmetic: 43.3 us -> none  [per_device(): source = jnp.zeros((station_count, cell_count), jnp.float32).at[:, flat_i...]
    select_n x7 -> x0, other arithmetic: 11.6 us -> none  [the longest x4 9.37 us: sweep_once(): return jnp.where(station_mask, 0.0, chosen)]
  transfers between devices with their start and end apart: 21 -> 0, of which waited for: 18 -> 0; matrix products, arithmetic and copies ran while one was open for 1% -> 0% of each run, Pallas kernels for 0% -> 0%
where the time goes in v1:
time: 101 us; the launch traced here: 100 us
  Pallas kernels  93.7 us (93%)
  local copies, waits for them, and re-layouts  5.52 us (5%)
    pallas_call x1, Pallas kernels, per_device(): pl.pallas_call(functools.partial(kernel, dims), out_shape=(jax.ShapeDtype...  93.7 us
    unnamed x12, local copies, waits for them, and re-layouts  5.44 us

profile of v1, /device:TPU:7, one launch (start us, length us, event | category | flops | bytes accessed | tf_op | source)
XLA Modules:
  0.0 100.0 jit_solution(3207391694050501292)
XLA Ops:
  0.6 0.0 copy-start.4
  0.6 0.6 copy-done.4
  1.3 0.0 copy-start.3
  1.3 0.7 copy-done.3
  2.0 0.1 convert_element_type.18
  2.1 0.1 bitcast_maximum_fusion.meta_ref
  2.2 0.0 copy-start
  2.2 1.0 %copy-done = f32[1,512,256]{2,1,0:T(8,128)S(1)} copy-done((f32[1,512,256]{2,1,0:T(8,128)S(1)}, f32[1,512,256]{2,1,0:T(8,128)}, u32[]{:S(2)}) %copy-start) | copy-done | bytes 524312
  3.2 0.0 copy-start.1
  3.2 0.9 copy-done.1
  4.1 0.0 copy-start.2
  4.1 0.8 copy-done.2
  4.9 93.7 %shard_map.68 = (f32[512,256]{1,0:T(8,128)S(1)}, f32[32,256]{1,0:T(8,128)S(1)}) custom-call(f32[512,256]{1,0:T(8,128)S(1)} %bitcast.11, f32[1,128]{1,0:T(1,128)S(1)} %bitcast_maximum_fusion.meta_ref, s32[3,8192]{1,0:T(4,128)S(1)} %copy-done.1, f32[1,8192]{1,0:T(1,128)S(1)} %copy-done.2), custom_call_target="tpu_custom_call" | custom-call | tf_op jit(solution)/shard_map/pallas_call | solution.py:480
  98.6 0.8 copy.9
  99.4 0.6 copy.10
  (4 shorter events, 0.0 us)
Async XLA Ops:
  0.6 0.7 copy-start.4
  1.3 0.7 copy-start.3
  2.2 1.0 %copy-start = (f32[1,512,256]{2,1,0:T(8,128)S(1)}, f32[1,512,256]{2,1,0:T(8,128)}, u32[]{:S(2)}) copy-start(f32[1,512,256]{2,1,0:T(8,128)} %param.5) | copy-start | bytes 1572868
  3.2 0.9 copy-start.1
  4.1 0.8 copy-start.2

commit v2 on v1

v2 whole, which is shorter than its diff:
```python
import functools

import jax
import jax.numpy as jnp
from jax import lax
from jax.experimental import pallas as pl
from jax.experimental.pallas import tpu as pltpu
from jax.sharding import PartitionSpec as P

TY = 32
BIG = 1000000.0
HALO = 8
GROUP = 2
MESH = pl.DeviceIdType.MESH


def godunov(near_x, near_y, near_z, cost):
    low_xy = jnp.minimum(near_x, near_y)
    high_xy = jnp.maximum(near_x, near_y)
    lowest = jnp.minimum(low_xy, near_z)
    rest = jnp.maximum(low_xy, near_z)
    middle = jnp.minimum(high_xy, rest)
    highest = jnp.maximum(high_xy, rest)
    gap2 = middle - lowest
    gap3 = highest - lowest
    cost_sq = cost * cost
    gap2_sq = gap2 * gap2
    disc2 = 2.0 * cost_sq - gap2_sq
    reach = gap3 + gap3 - gap2
    two = disc2 <= reach * reach
    step = gap3 - gap2
    disc3 = 3.0 * cost_sq - (gap2_sq + gap3 * gap3 + step * step)
    disc = jnp.where(two, disc2, disc3)
    base = jnp.where(two, gap2, gap2 + gap3)
    scale = jnp.where(two, 0.5, 1.0 / 3.0)
    wide = lowest + (base + root(jnp.maximum(disc, 1e-30))) * scale
    return jnp.where(cost <= gap2, lowest + cost, wide)


def tiles_of(ref, index):
    return {
        (t, h): ref[index + (pl.ds(8 * t, 8), pl.ds(128 * h, 128))]
        for t in range(ref.shape[-2] // 8)
        for h in range(ref.shape[-1] // 128)
    }


def at_tile(t, h):
    return (pl.ds(8 * t, 8), pl.ds(128 * h, 128))


def beside_x(field, fill):
    sub = lax.broadcasted_iota(jnp.int32, (8, 128), 0)
    down = {key: pltpu.roll(value, 1, 0) for key, value in field.items()}
    up = {key: pltpu.roll(value, 7, 0) for key, value in field.items()}
    low = {(t, h): jnp.where(sub == 0, down.get((t - 1, h), fill), down[t, h]) for t, h in field}
    high = {(t, h): jnp.where(sub == 7, up.get((t + 1, h), fill), up[t, h]) for t, h in field}
    return low, high


def beside_z(field, fill):
    lane = lax.broadcasted_iota(jnp.int32, (8, 128), 1)
    down = {key: pltpu.roll(value, 1, 1) for key, value in field.items()}
    up = {key: pltpu.roll(value, 127, 1) for key, value in field.items()}
    low = {(t, h): jnp.where(lane == 0, down.get((t, h - 1), fill), down[t, h]) for t, h in field}
    high = {(t, h): jnp.where(lane == 127, up.get((t, h + 1), fill), up[t, h]) for t, h in field}
    return low, high


def root(value):
    return value * lax.rsqrt(jnp.maximum(value, 1e-30))


def kernel(
    dims,
    velocity_ref,
    meta_ref,
    events_hbm,
    delays_ref,
    times_out,
    kernel_out,
    events_ref,
    vel,
    slow,
    meta,
    delay,
    start,
    time_a,
    time_b,
    count,
    late,
    masks,
    spot,
    weights,
    source,
    adj_a,
    adj_b,
    dens,
    part,
    parts,
    total,
    local_sem,
    send_sem,
    recv_sem,
    last_sem,
):
    n_src, n_space, ny, nz, events = dims
    group = GROUP
    rows = ny // (n_space * group)
    peers = n_src // group
    chunk_x = n_space // peers
    own_rows = ny // n_src
    per_owner = own_rows // rows
    tall = rows + 2 * HALO
    s, p = lax.axis_index("src"), lax.axis_index("space")
    m, g = s // group, s % group
    block = g * n_space + p
    y_base = block * rows
    n_blocks = n_space * group

    def where_is(b):
        return (m * group + b // n_space, b % n_space)

    owner = block // per_owner
    targets = [(owner, chunk_x * m + k) for k in range(chunk_x)]
    sources = []
    for k in range(per_owner):
        b = s * per_owner + k
        sources.append(((p // chunk_x) * group + b // n_space, b % n_space))

    fetch_events = pltpu.make_async_copy(events_hbm, events_ref, local_sem)
    fetch_events.start()

    barrier = pltpu.get_barrier_semaphore()
    signals = 0
    for i in range(1, n_space):
        to = (s, (p + i) % n_space)
        pl.semaphore_signal(barrier, inc=1, device_id=to, device_id_type=MESH)
        signals += 1
    for dg in range(1, group):
        to = (m * group + (g + dg) % group, p)
        pl.semaphore_signal(barrier, inc=1, device_id=to, device_id_type=MESH)
        signals += 1
    for i in range(1, peers):
        to = (((m + i) % peers) * group + g, p)
        pl.semaphore_signal(barrier, inc=1, device_id=to, device_id_type=MESH)
        signals += 1
    for to in sources:
        mine = (to[0] == s) & (to[1] == p)

        @pl.when(jnp.logical_not(mine))
        def _():
            pl.semaphore_signal(barrier, inc=1, device_id=to, device_id_type=MESH)

        signals = signals + jnp.where(mine, 0, 1)
    pl.semaphore_wait(barrier, signals)

    own = pl.ds(HALO, rows)
    partners = [(m * group + (g + dg) % group, p) for dg in range(1, group)]
    for i in range(n_space):
        q = (p + i) % n_space
        line = meta.at[g, pl.ds(p, 1), :]
        if i == 0:
            pltpu.make_async_copy(meta_ref, line, recv_sem.at[1]).start()
        else:
            pltpu.make_async_remote_copy(
                meta_ref,
                line,
                send_sem.at[1],
                recv_sem.at[1],
                device_id=(s, q),
                device_id_type=MESH,
            ).start()
    for i in range(n_space):
        q = (p + i) % n_space
        piece = velocity_ref.at[pl.ds(pl.multiple_of((g * n_space + q) * rows, 8), rows), :]
        if i == 0:
            pltpu.make_async_copy(piece, vel.at[own, p, :], recv_sem.at[0]).start()
        else:
            pltpu.make_async_remote_copy(
                piece,
                vel.at[own, p, :],
                send_sem.at[0],
                recv_sem.at[0],
                device_id=(s, q),
                device_id_type=MESH,
            ).start()
    pltpu.make_async_copy(delays_ref, delay.at[g], recv_sem.at[2]).start()
    for to in partners:
        pltpu.make_async_remote_copy(
            delays_ref,
            delay.at[g],
            send_sem.at[2],
            recv_sem.at[2],
            device_id=to,
            device_id_type=MESH,
        ).start()

    src_rows = rows + 10
    cells = src_rows * n_space
    step_events = 1024
    steps = events // step_events
    count[...] = jnp.zeros_like(count)
    late[...] = jnp.zeros_like(late)
    fetch_events.wait()
    pltpu.make_async_copy(delay, delay, recv_sem.at[2]).wait()

    def add_events(c, carry):
        at = pl.ds(pl.multiple_of(c * step_events, step_events), step_events)
        event_x = events_ref[0:1, at]
        event_y = events_ref[1:2, at]
        event_z = events_ref[2:3, at]
        key = (event_y - (y_base - 5)) * n_space + event_x
        cell = lax.broadcasted_iota(jnp.int32, (cells, step_events), 0)
        left = jnp.where(cell == key, 1.0, 0.0).astype(jnp.bfloat16)
        deep = lax.broadcasted_iota(jnp.int32, (nz, step_events), 0) == event_z
        contract = (((1,), (1,)), ((), ()))

        def product(value):
            right = jnp.where(deep, value, 0.0).astype(jnp.bfloat16)
            return lax.dot_general(left, right, contract, preferred_element_type=jnp.float32)

        count[...] += product(1.0)
        for k in range(group):
            lateness = delay[k, 0:1, at]
            coarse = lateness.astype(jnp.bfloat16).astype(jnp.float32)
            late[k] += product(coarse) + product(lateness - coarse)
        return carry

    cut_a, cut_b = (steps * 3) // 8, (steps * 5) // 8
    lax.fori_loop(0, cut_a, add_events, 0)

    pltpu.make_async_copy(meta.at[g], meta.at[g], recv_sem.at[1]).wait()
    for to in partners:
        pltpu.make_async_remote_copy(
            meta.at[g],
            meta.at[g],
            send_sem.at[3],
            recv_sem.at[3],
            device_id=to,
            device_id_type=MESH,
        ).start()
    lax.fori_loop(cut_a, cut_b, add_events, 0)

    pltpu.make_async_copy(vel.at[own], vel.at[own], recv_sem.at[0]).wait()
    for dg in range(1, group):
        other = (g + dg) % group
        pltpu.make_async_copy(meta.at[other], meta.at[other], recv_sem.at[3]).wait()
    before = where_is((block + n_blocks - 1) % n_blocks)
    after = where_is((block + 1) % n_blocks)
    to_before = pltpu.make_async_remote_copy(
        vel.at[pl.ds(HALO, HALO)],
        vel.at[pl.ds(HALO + rows, HALO)],
        send_sem.at[4],
        recv_sem.at[4],
        device_id=before,
        device_id_type=MESH,
    )
    to_after = pltpu.make_async_remote_copy(
        vel.at[pl.ds(rows, HALO)],
        vel.at[pl.ds(0, HALO)],
        send_sem.at[5],
        recv_sem.at[5],
        device_id=after,
        device_id_type=MESH,
    )
    to_before.start()
    to_after.start()
    lax.fori_loop(cut_b, steps, add_events, 0)

    lane = lax.broadcasted_iota(jnp.int32, (n_space, 128), 1)
    layer_f = lax.broadcasted_iota(jnp.int32, (n_space, nz), 0).astype(jnp.float32)
    depth_f = lax.broadcasted_iota(jnp.int32, (n_space, nz), 1).astype(jnp.float32)
    first_tile = (y_base - HALO + TY) // TY - 1
    tile_count = ny // TY

    def column(k, index):
        picked = jnp.where(lane == index, meta[k], 0.0)
        return jnp.broadcast_to(jnp.sum(picked, axis=1, keepdims=True), (n_space, nz))

    def row_valid(y):
        return (y >= 0) & (y < ny)

    for k in range(group):
        for r in range(2):
            for t in range(2):
                masks[r, k, t] = column(k, r * tile_count + first_tile + t)
            masks[r, k, 2] = jnp.zeros((n_space, nz), jnp.float32)
        cell_x, cell_y, cell_z = column(k, 64), column(k, 65), column(k, 66)
        here = (layer_f == cell_x) & (depth_f == cell_z)
        spot[k] = jnp.where(here, cell_y, -1.0)
        flat = (layer_f - cell_x) * (layer_f - cell_x) + (depth_f - cell_z) * (depth_f - cell_z)

        def init_row(j, carry):
            y = y_base - HALO - 1 + j
            diff = y.astype(jnp.float32) - cell_y
            start[k, j] = jnp.where(row_valid(y), root(flat + diff * diff), BIG)
            return carry

        lax.fori_loop(0, tall + 2, init_row, 0, unroll=2)

    to_before.wait_recv()
    to_after.wait_recv()

    def slow_row(j, carry):
        slow[j] = 1.0 / vel[j]
        return carry

    lax.fori_loop(0, tall, slow_row, 0, unroll=4)

    def sweep(old, new, low, high, r):
        def row(j, carry):
            y = y_base - HALO + j
            kind = jnp.where(row_valid(y), (y + TY) // TY - 1 - first_tile, 2)
            for k in range(group):
                centre = tiles_of(old, (k, j + 1))
                x_low, x_high = beside_x(centre, BIG)
                z_low, z_high = beside_z(centre, BIG)
                for t, h in centre:
                    tile = at_tile(t, h)
                    update = godunov(
                        jnp.minimum(x_low[t, h], x_high[t, h]),
                        jnp.minimum(old[(k, j) + tile], old[(k, j + 2) + tile]),
                        jnp.minimum(z_low[t, h], z_high[t, h]),
                        slow[(j,) + tile],
                    )
                    chosen = (masks[(r, k, kind) + tile] > 0.0) & (
                        spot[(k,) + tile] != y.astype(jnp.float32)
                    )
                    new[(k, j + 1) + tile] = jnp.where(chosen, update, centre[t, h])
            return carry

        lax.fori_loop(low, high, row, 0, unroll=4)

    inner = pl.ds(HALO + 1, rows)
    sweep(start, time_a, 0, tall, 0)
    sweep(time_a, time_b, 1, tall - 1, 0)
    sweep(time_b, time_a, 2, tall - 2, 1)
    sweep(time_a, time_b, 3, tall - 3, 1)
    for k in range(group):
        for i in range(n_space):
            q = (p + i) % n_space
            piece = time_b.at[k, inner, q, :]
            place = times_out.at[pl.ds(pl.multiple_of(y_base, 8), rows), :]
            to_src = m * group + k

            def send(piece=piece, place=place, to_src=to_src, q=q):
                pltpu.make_async_remote_copy(
                    piece,
                    place,
                    send_sem.at[6],
                    recv_sem.at[6],
                    device_id=(to_src, q),
                    device_id_type=MESH,
                ).start()

            if i:
                send()
            else:

                @pl.when(g == k)
                def _():
                    pltpu.make_async_copy(piece, place, recv_sem.at[6]).start()

                @pl.when(g != k)
                def _():
                    send()

    def source_row(i, carry):
        at = pl.ds(pl.multiple_of(i * n_space, n_space), n_space)
        for k in range(group):
            shift = time_b[k, i + 4] - start[k, i + 4]
            source[k, i] = count[at, :] * shift - late[k, at, :]
        return carry

    lax.fori_loop(0, src_rows, source_row, 0, unroll=2)

    def weight_row(i, carry):
        j = i + 5
        for k in range(group):
            centre = tiles_of(time_b, (k, j))
            x_low, x_high = beside_x(centre, 0.0)
            z_low, z_high = beside_z(centre, 0.0)
            for t, h in centre:
                tile = at_tile(t, h)
                rate = vel[(i + 4,) + tile] * (1.0 / 6.0)
                around = (
                    x_low[t, h],
                    x_high[t, h],
                    time_b[(k, j - 1) + tile],
                    time_b[(k, j + 1) + tile],
                    z_low[t, h],
                    z_high[t, h],
                )
                for d, near in enumerate(around):
                    weights[(k, d, i) + tile] = jnp.maximum(near - centre[t, h], 0.0) * rate
        return carry

    lax.fori_loop(0, src_rows - 2, weight_row, 0, unroll=4)

    def adjoint_sweep(old, new, low, high):
        def row(i, carry):
            for k in range(group):
                centre = tiles_of(old, (k, i))
                x_low, x_high = beside_x(centre, 0.0)
                z_low, z_high = beside_z(centre, 0.0)
                for t, h in centre:
                    tile = at_tile(t, h)
                    weight = [weights[(k, d, i - 1) + tile] for d in range(6)]
                    along_x = weight[0] * x_low[t, h] + weight[1] * x_high[t, h]
                    along_y = weight[2] * old[(k, i - 1) + tile] + weight[3] * old[(k, i + 1) + tile]
                    along_z = weight[4] * z_low[t, h] + weight[5] * z_high[t, h]
                    new[(k, i) + tile] = source[(k, i) + tile] + along_x + (along_y + along_z)
            return carry

        lax.fori_loop(low, high, row, 0, unroll=4)

    adjoint_sweep(source, adj_a, 1, src_rows - 1)
    adjoint_sweep(adj_a, adj_b, 2, src_rows - 2)
    adjoint_sweep(adj_b, adj_a, 3, src_rows - 3)
    adjoint_sweep(adj_a, adj_b, 4, src_rows - 4)

    def density_row(i, carry):
        value = adj_b[0, i + 4]
        for k in range(1, group):
            value = value + adj_b[k, i + 4]
        dens[i] = slow[i + HALO - 1] * value
        return carry

    lax.fori_loop(0, rows + 2, density_row, 0, unroll=2)

    def smooth_row(i, carry):
        first, middle, last = (tiles_of(dens, (i + d,)) for d in range(3))
        value = {key: first[key] + 2.0 * middle[key] + last[key] for key in first}
        for beside in (beside_x, beside_z):
            low, high = beside(value, 0.0)
            value = {key: low[key] + 2.0 * value[key] + high[key] for key in value}
        for t, h in value:
            part[(i,) + at_tile(t, h)] = value[t, h] * (1.0 / 64.0)
        return carry

    lax.fori_loop(0, rows, smooth_row, 0, unroll=2)

    for i in range(peers):
        q = (m + i) % peers
        piece = part.at[:, pl.ds(pl.multiple_of(q * chunk_x, chunk_x), chunk_x), :]
        if i == 0:
            pltpu.make_async_copy(piece, parts.at[m], recv_sem.at[7]).start()
        else:
            pltpu.make_async_remote_copy(
                piece,
                parts.at[m],
                send_sem.at[7],
                recv_sem.at[7],
                device_id=(q * group + g, p),
                device_id_type=MESH,
            ).start()
    pltpu.make_async_copy(parts, parts, recv_sem.at[7]).wait()
    summed = parts[0]
    for i in range(1, peers):
        summed = summed + parts[i]
    total[...] = summed
    place_k = block % per_owner
    for k in range(chunk_x):
        to = targets[k]
        piece = total.at[:, k, :]
        place = kernel_out.at[pl.ds(pl.multiple_of(place_k * rows, 8), rows), :]
        mine = (to[0] == s) & (to[1] == p)

        @pl.when(mine)
        def _():
            pltpu.make_async_copy(piece, place, recv_sem.at[8]).start()

        @pl.when(jnp.logical_not(mine))
        def _():
            pltpu.make_async_remote_copy(
                piece,
                place,
                last_sem.at[k],
                recv_sem.at[8],
                device_id=to,
                device_id_type=MESH,
            ).start()

    def drain(ref, sem):
        pltpu.make_async_copy(ref, ref, sem).wait()

    drain(velocity_ref.at[pl.ds(0, (n_space - 1) * rows), :], send_sem.at[0])
    drain(meta.at[0, pl.ds(0, n_space - 8), :], send_sem.at[1])
    for _ in range(7):
        drain(meta_ref, send_sem.at[1])
    for _ in partners:
        drain(delay.at[0], send_sem.at[2])
        drain(meta.at[0], send_sem.at[3])
    to_before.wait_send()
    to_after.wait_send()
    drain(times_out.at[pl.ds(0, (n_blocks - 1) * rows), :], send_sem.at[6])
    drain(parts.at[pl.ds(1, peers - 1)], send_sem.at[7])
    for k in range(chunk_x):
        to = targets[k]
        mine = (to[0] == s) & (to[1] == p)

        @pl.when(jnp.logical_not(mine))
        def _():
            drain(total.at[:, k, :], last_sem.at[k])

    drain(times_out, recv_sem.at[6])
    drain(kernel_out, recv_sem.at[8])


def per_device(dims, velocity, station_cells, event_cells, delays, active):
    n_src, n_space, ny, nz, events = dims
    rows = ny // (n_space * GROUP)
    tall = rows + 2 * HALO
    peers = n_src // GROUP
    chunk_x = n_space // peers
    own_rows = ny // n_src
    src_rows = rows + 10
    flags = active.reshape(1, -1).astype(jnp.float32)
    cells = station_cells.astype(jnp.float32)
    meta = jnp.concatenate(
        [
            flags,
            jnp.zeros((1, 64 - flags.shape[1]), jnp.float32),
            cells,
            jnp.zeros((1, 61), jnp.float32),
        ],
        axis=1,
    )
    f32 = jnp.float32
    plane = (n_space, nz)
    vmem = pl.BlockSpec(memory_space=pltpu.VMEM)
    anywhere = pl.BlockSpec(memory_space=pl.ANY)
    hbm = pl.BlockSpec(memory_space=pltpu.HBM)
    times, kernel_part = pl.pallas_call(
        functools.partial(kernel, dims),
        out_shape=(
            jax.ShapeDtypeStruct((ny, nz), f32),
            jax.ShapeDtypeStruct((own_rows, nz), f32),
        ),
        in_specs=[hbm, vmem, hbm, hbm],
        out_specs=(anywhere, anywhere),
        scratch_shapes=[
            pltpu.VMEM((3, events), jnp.int32),
            pltpu.VMEM((tall,) + plane, f32),
            pltpu.VMEM((tall,) + plane, f32),
            pltpu.VMEM((GROUP, n_space, 128), f32),
            pltpu.VMEM((GROUP, 1, events), f32),
            pltpu.VMEM((GROUP, tall + 2) + plane, f32),
            pltpu.VMEM((GROUP, tall + 2) + plane, f32),
            pltpu.VMEM((GROUP, tall + 2) + plane, f32),
            pltpu.VMEM((src_rows * n_space, nz), f32),
            pltpu.VMEM((GROUP, src_rows * n_space, nz), f32),
            pltpu.VMEM((2, GROUP, 3) + plane, f32),
            pltpu.VMEM((GROUP,) + plane, f32),
            pltpu.VMEM((GROUP, 6, src_rows - 2) + plane, f32),
            pltpu.VMEM((GROUP, src_rows) + plane, f32),
            pltpu.VMEM((GROUP, src_rows) + plane, f32),
            pltpu.VMEM((GROUP, src_rows) + plane, f32),
            pltpu.VMEM((rows + 2,) + plane, f32),
            pltpu.VMEM((rows,) + plane, f32),
            pltpu.VMEM((peers, rows, chunk_x, nz), f32),
            pltpu.VMEM((rows, chunk_x, nz), f32),
            pltpu.SemaphoreType.DMA,
            pltpu.SemaphoreType.DMA((8,)),
            pltpu.SemaphoreType.DMA((9,)),
            pltpu.SemaphoreType.DMA((chunk_x,)),
        ],
        compiler_params=pltpu.CompilerParams(
            collective_id=0, has_side_effects=True, vmem_limit_bytes=60 << 20
        ),
    )(velocity[0], meta, event_cells, delays)
    return times[None, None], kernel_part[None]


def solution(mesh):
    n_src, n_space = mesh.shape["src"], mesh.shape["space"]

    def run(velocity, station_cells, event_cells, delays, active):
        dims = (n_src, n_space, velocity.shape[1], velocity.shape[2], event_cells.shape[1])
        return jax.shard_map(
            functools.partial(per_device, dims),
            mesh=mesh,
            in_specs=(
                P("space", None, None),
                P("src", None),
                P(),
                P("src", None),
                P(None, "src", "space", None),
            ),
            out_specs=(P("src", "space", None, None), P("space", "src", None)),
            check_vma=False,
        )(velocity, station_cells, event_cells, delays, active)

    return run
```

time: 101 us -> 72.1 us (0.71)
  Pallas kernels: 93.7 us -> 66.7 us
  local copies, waits for them, and re-layouts: 5.52 us -> 3.9 us
    pallas_call x1, Pallas kernels: 93.7 us -> 66.7 us  [per_device(): pl.pallas_call(functools.partial(kernel, dims), out_shape=(jax.ShapeDtype...]
    unnamed x12 -> x8, local copies, waits for them, and re-layouts: 5.44 us -> 3.82 us
where the time goes in v2:
time: 72.1 us; the launch traced here: 71.9 us
  Pallas kernels  66.7 us (93%)
  local copies, waits for them, and re-layouts  3.9 us (5%)
    pallas_call x1, Pallas kernels, per_device(): pl.pallas_call(functools.partial(kernel, dims), out_shape=(jax.ShapeDtype...  66.7 us
    unnamed x8, local copies, waits for them, and re-layouts  3.82 us

profile of v2, /device:TPU:7, one launch (start us, length us, event | category | flops | bytes accessed | tf_op | source)
XLA Modules:
  0.0 71.9 jit_solution(6876944602656875806)
XLA Ops:
  0.6 0.0 copy-start.2
  0.6 0.6 copy-done.2
  1.3 0.0 copy-start.1
  1.3 0.7 copy-done.1
  2.0 0.1 convert_element_type.18
  2.1 0.6 bitcast_maximum_fusion.meta_ref
  2.7 66.7 %shard_map.68 = (f32[512,256]{1,0:T(8,128)}, f32[32,256]{1,0:T(8,128)}) custom-call(f32[512,256]{1,0:T(8,128)} %bitcast.11, f32[1,128]{1,0:T(1,128)} %bitcast_maximum_fusion.meta_ref, s32[3,8192]{1,0:T(4,128)} %events_hbm.1, f32[1,8192]{1,0:T(1,128)} %delays_ref.1), custom_call_target="tpu_custom_call" | custom-call | tf_op jit(solution)/shard_map/pallas_call | solution.py:535
  69.4 0.0 copy-start
  69.4 1.9 %copy.9 = f32[1,1,512,256]{3,2,1,0:T(8,128)} copy(f32[1,1,512,256]{3,2,1,0:T(8,128)} %bitcast.12) | data formatting | bytes 1048576
  71.3 0.0 copy-done
  71.3 0.6 copy.10
  (4 shorter events, 0.0 us)
Async XLA Ops:
  0.6 0.7 copy-start.2
  1.3 0.7 copy-start.1
  69.4 1.9 %copy-start = (f32[32,256]{1,0:T(8,128)S(1)}, f32[32,256]{1,0:T(8,128)}, u32[]{:S(2)}) copy-start(f32[32,256]{1,0:T(8,128)} %get-tuple-element.5) | copy-start | bytes 98308

commit v3 on v2

--- a/solution.py
+++ b/solution.py
@@ -74,11 +74,13 @@
 def kernel(
     dims,
     velocity_ref,
-    meta_ref,
+    cells_ref,
+    flags_ref,
     events_hbm,
     delays_ref,
     times_out,
     kernel_out,
+    meta_ref,
     events_ref,
     vel,
     slow,
@@ -87,8 +89,7 @@
     start,
     time_a,
     time_b,
-    count,
-    late,
+    landed,
     masks,
     spot,
     weights,
@@ -102,6 +103,8 @@
     local_sem,
     send_sem,
     recv_sem,
+    halo_send,
+    halo_recv,
     last_sem,
 ):
     n_src, n_space, ny, nz, events = dims
@@ -130,6 +133,17 @@
 
     fetch_events = pltpu.make_async_copy(events_hbm, events_ref, local_sem)
     fetch_events.start()
+
+    lane = lax.broadcasted_iota(jnp.int32, (1, 128), 1)
+    line = jnp.zeros((1, 128), jnp.float32)
+    tile_count = ny // TY
+    for r in range(2):
+        for t in range(tile_count):
+            flag = flags_ref[r, t].astype(jnp.float32)
+            line = jnp.where(lane == r * tile_count + t, flag, line)
+    for d in range(3):
+        line = jnp.where(lane == 64 + d, cells_ref[0, d].astype(jnp.float32), line)
+    meta_ref[...] = line
 
     barrier = pltpu.get_barrier_semaphore()
     signals = 0
@@ -171,17 +185,24 @@
                 device_id=(s, q),
                 device_id_type=MESH,
             ).start()
+    half = n_space // 2
+    near_half = (p // half) * half
+    far_half = half - near_half
     for i in range(n_space):
-        q = (p + i) % n_space
+        if i < half:
+            q = near_half + (p + i) % half
+        else:
+            q = far_half + (p + i) % half
         piece = velocity_ref.at[pl.ds(pl.multiple_of((g * n_space + q) * rows, 8), rows), :]
+        arrived = recv_sem.at[0] if i < half else recv_sem.at[9]
         if i == 0:
-            pltpu.make_async_copy(piece, vel.at[own, p, :], recv_sem.at[0]).start()
+            pltpu.make_async_copy(piece, vel.at[own, p, :], arrived).start()
         else:
             pltpu.make_async_remote_copy(
                 piece,
                 vel.at[own, p, :],
                 send_sem.at[0],
-                recv_sem.at[0],
+                arrived,
                 device_id=(s, q),
                 device_id_type=MESH,
             ).start()
@@ -197,11 +218,11 @@
         ).start()
 
     src_rows = rows + 10
-    cells = src_rows * n_space
+    cells = rows * n_space
     step_events = 1024
     steps = events // step_events
-    count[...] = jnp.zeros_like(count)
-    late[...] = jnp.zeros_like(late)
+    mine_rows = pl.ds(5, rows)
+    landed[mine_rows] = jnp.zeros((rows, 1 + group, n_space, nz), jnp.float32)
     fetch_events.wait()
     pltpu.make_async_copy(delay, delay, recv_sem.at[2]).wait()
 
@@ -210,7 +231,7 @@
         event_x = events_ref[0:1, at]
         event_y = events_ref[1:2, at]
         event_z = events_ref[2:3, at]
-        key = (event_y - (y_base - 5)) * n_space + event_x
+        key = (event_y - y_base) * n_space + event_x
         cell = lax.broadcasted_iota(jnp.int32, (cells, step_events), 0)
         left = jnp.where(cell == key, 1.0, 0.0).astype(jnp.bfloat16)
         deep = lax.broadcasted_iota(jnp.int32, (nz, step_events), 0) == event_z
@@ -218,17 +239,55 @@
 
         def product(value):
             right = jnp.where(deep, value, 0.0).astype(jnp.bfloat16)
-            return lax.dot_general(left, right, contract, preferred_element_type=jnp.float32)
-
-        count[...] += product(1.0)
+            out = lax.dot_general(left, right, contract, preferred_element_type=jnp.float32)
+            return out.reshape(rows, n_space, nz)
+
+        landed[mine_rows, 0] += product(1.0)
         for k in range(group):
             lateness = delay[k, 0:1, at]
             coarse = lateness.astype(jnp.bfloat16).astype(jnp.float32)
-            late[k] += product(coarse) + product(lateness - coarse)
+            landed[mine_rows, 1 + k] += product(coarse) + product(lateness - coarse)
         return carry
 
-    cut_a, cut_b = (steps * 3) // 8, (steps * 5) // 8
-    lax.fori_loop(0, cut_a, add_events, 0)
+    wide_lane = lax.broadcasted_iota(jnp.int32, (n_space, 128), 1)
+    layer_f = lax.broadcasted_iota(jnp.int32, (n_space, nz), 0).astype(jnp.float32)
+    depth_f = lax.broadcasted_iota(jnp.int32, (n_space, nz), 1).astype(jnp.float32)
+    first_tile = (y_base - HALO + TY) // TY - 1
+
+    def column(k, index):
+        picked = jnp.where(wide_lane == index, meta[k], 0.0)
+        return jnp.broadcast_to(jnp.sum(picked, axis=1, keepdims=True), (n_space, nz))
+
+    def row_valid(y):
+        return (y >= 0) & (y < ny)
+
+    def init_fields():
+        for dg in range(1, group):
+            other = (g + dg) % group
+            pltpu.make_async_copy(meta.at[other], meta.at[other], recv_sem.at[3]).wait()
+        for k in range(group):
+            for r in range(2):
+                for t in range(2):
+                    masks[r, k, t] = column(k, r * tile_count + first_tile + t)
+                masks[r, k, 2] = jnp.zeros((n_space, nz), jnp.float32)
+            cell_x, cell_y, cell_z = column(k, 64), column(k, 65), column(k, 66)
+            here = (layer_f == cell_x) & (depth_f == cell_z)
+            spot[k] = jnp.where(here, cell_y, -1.0)
+            off_x, off_z = layer_f - cell_x, depth_f - cell_z
+            flat = off_x * off_x + off_z * off_z
+
+            def init_row(j, carry):
+                y = y_base - HALO - 1 + j
+                diff = y.astype(jnp.float32) - cell_y
+                start[k, j] = jnp.where(row_valid(y), root(flat + diff * diff), BIG)
+                return carry
+
+            lax.fori_loop(0, tall + 2, init_row, 0, unroll=2)
+
+    before = where_is((block + n_blocks - 1) % n_blocks)
+    after = where_is((block + 1) % n_blocks)
+    cut = steps // 2
+    lax.fori_loop(0, cut, add_events, 0)
 
     pltpu.make_async_copy(meta.at[g], meta.at[g], recv_sem.at[1]).wait()
     for to in partners:
@@ -240,104 +299,98 @@
             device_id=to,
             device_id_type=MESH,
         ).start()
-    lax.fori_loop(cut_a, cut_b, add_events, 0)
-
-    pltpu.make_async_copy(vel.at[own], vel.at[own], recv_sem.at[0]).wait()
-    for dg in range(1, group):
-        other = (g + dg) % group
-        pltpu.make_async_copy(meta.at[other], meta.at[other], recv_sem.at[3]).wait()
-    before = where_is((block + n_blocks - 1) % n_blocks)
-    after = where_is((block + 1) % n_blocks)
-    to_before = pltpu.make_async_remote_copy(
-        vel.at[pl.ds(HALO, HALO)],
-        vel.at[pl.ds(HALO + rows, HALO)],
+    lax.fori_loop(cut, steps, add_events, 0)
+
+    halos = []
+    for n, (x_at, arrived) in enumerate(((near_half, 0), (far_half, 9))):
+        layers = pl.ds(pl.multiple_of(x_at, half), half)
+        here = vel.at[own, layers, :]
+        pltpu.make_async_copy(here, here, recv_sem.at[arrived]).wait()
+        for d, (at, there, to) in enumerate(
+            ((HALO, HALO + rows, before), (rows, 0, after))
+        ):
+            halo = pltpu.make_async_remote_copy(
+                vel.at[pl.ds(at, HALO), layers, :],
+                vel.at[pl.ds(there, HALO), layers, :],
+                halo_send.at[2 * n + d],
+                halo_recv.at[2 * n + d],
+                device_id=to,
+                device_id_type=MESH,
+            )
+            halo.start()
+            halos.append(halo)
+        if n == 0:
+            init_fields()
+
+    events_before = pltpu.make_async_remote_copy(
+        landed.at[pl.ds(5, 5)],
+        landed.at[pl.ds(5 + rows, 5)],
         send_sem.at[4],
         recv_sem.at[4],
         device_id=before,
         device_id_type=MESH,
     )
-    to_after = pltpu.make_async_remote_copy(
-        vel.at[pl.ds(rows, HALO)],
-        vel.at[pl.ds(0, HALO)],
+    events_after = pltpu.make_async_remote_copy(
+        landed.at[pl.ds(rows, 5)],
+        landed.at[pl.ds(0, 5)],
         send_sem.at[5],
         recv_sem.at[5],
         device_id=after,
         device_id_type=MESH,
     )
-    to_before.start()
-    to_after.start()
-    lax.fori_loop(cut_b, steps, add_events, 0)
-
-    lane = lax.broadcasted_iota(jnp.int32, (n_space, 128), 1)
-    layer_f = lax.broadcasted_iota(jnp.int32, (n_space, nz), 0).astype(jnp.float32)
-    depth_f = lax.broadcasted_iota(jnp.int32, (n_space, nz), 1).astype(jnp.float32)
-    first_tile = (y_base - HALO + TY) // TY - 1
-    tile_count = ny // TY
-
-    def column(k, index):
-        picked = jnp.where(lane == index, meta[k], 0.0)
-        return jnp.broadcast_to(jnp.sum(picked, axis=1, keepdims=True), (n_space, nz))
-
-    def row_valid(y):
-        return (y >= 0) & (y < ny)
-
-    for k in range(group):
-        for r in range(2):
-            for t in range(2):
-                masks[r, k, t] = column(k, r * tile_count + first_tile + t)
-            masks[r, k, 2] = jnp.zeros((n_space, nz), jnp.float32)
-        cell_x, cell_y, cell_z = column(k, 64), column(k, 65), column(k, 66)
-        here = (layer_f == cell_x) & (depth_f == cell_z)
-        spot[k] = jnp.where(here, cell_y, -1.0)
-        flat = (layer_f - cell_x) * (layer_f - cell_x) + (depth_f - cell_z) * (depth_f - cell_z)
-
-        def init_row(j, carry):
-            y = y_base - HALO - 1 + j
-            diff = y.astype(jnp.float32) - cell_y
-            start[k, j] = jnp.where(row_valid(y), root(flat + diff * diff), BIG)
-            return carry
-
-        lax.fori_loop(0, tall + 2, init_row, 0, unroll=2)
-
-    to_before.wait_recv()
-    to_after.wait_recv()
 
     def slow_row(j, carry):
         slow[j] = 1.0 / vel[j]
         return carry
 
-    lax.fori_loop(0, tall, slow_row, 0, unroll=4)
-
-    def sweep(old, new, low, high, r):
-        def row(j, carry):
-            y = y_base - HALO + j
-            kind = jnp.where(row_valid(y), (y + TY) // TY - 1 - first_tile, 2)
-            for k in range(group):
-                centre = tiles_of(old, (k, j + 1))
-                x_low, x_high = beside_x(centre, BIG)
-                z_low, z_high = beside_z(centre, BIG)
-                for t, h in centre:
-                    tile = at_tile(t, h)
-                    update = godunov(
-                        jnp.minimum(x_low[t, h], x_high[t, h]),
-                        jnp.minimum(old[(k, j) + tile], old[(k, j + 2) + tile]),
-                        jnp.minimum(z_low[t, h], z_high[t, h]),
-                        slow[(j,) + tile],
-                    )
-                    chosen = (masks[(r, k, kind) + tile] > 0.0) & (
-                        spot[(k,) + tile] != y.astype(jnp.float32)
-                    )
-                    new[(k, j + 1) + tile] = jnp.where(chosen, update, centre[t, h])
+    def sweep_row(old, new, r, j):
+        y = y_base - HALO + j
+        kind = jnp.where(row_valid(y), (y + TY) // TY - 1 - first_tile, 2)
+        for k in range(group):
+            centre = tiles_of(old, (k, j + 1))
+            x_low, x_high = beside_x(centre, BIG)
+            z_low, z_high = beside_z(centre, BIG)
+            for t, h in centre:
+                tile = at_tile(t, h)
+                update = godunov(
+                    jnp.minimum(x_low[t, h], x_high[t, h]),
+                    jnp.minimum(old[(k, j) + tile], old[(k, j + 2) + tile]),
+                    jnp.minimum(z_low[t, h], z_high[t, h]),
+                    slow[(j,) + tile],
+                )
+                chosen = (masks[(r, k, kind) + tile] > 0.0) & (
+                    spot[(k,) + tile] != y.astype(jnp.float32)
+                )
+                new[(k, j + 1) + tile] = jnp.where(chosen, update, centre[t, h])
+
+    stages = ((start, time_a, 0), (time_a, time_b, 0), (time_b, time_a, 1), (time_a, time_b, 1))
+    lax.fori_loop(HALO, HALO + rows, slow_row, 0, unroll=4)
+    for n, (old, new, r) in enumerate(stages):
+
+        def inside(j, carry):
+            sweep_row(old, new, r, j)
             return carry
 
-        lax.fori_loop(low, high, row, 0, unroll=4)
+        lax.fori_loop(HALO + n, HALO + rows - n, inside, 0, unroll=2)
+
+    for halo in halos:
+        halo.wait_recv()
+    events_before.start()
+    events_after.start()
+    lax.fori_loop(0, HALO, slow_row, 0, unroll=4)
+    lax.fori_loop(HALO + rows, tall, slow_row, 0, unroll=4)
+    for n, (old, new, r) in enumerate(stages):
+
+        def outside(i, carry):
+            sweep_row(old, new, r, n + i)
+            sweep_row(old, new, r, HALO + rows - n + i)
+            return carry
+
+        lax.fori_loop(0, HALO, outside, 0, unroll=2)
 
     inner = pl.ds(HALO + 1, rows)
-    sweep(start, time_a, 0, tall, 0)
-    sweep(time_a, time_b, 1, tall - 1, 0)
-    sweep(time_b, time_a, 2, tall - 2, 1)
-    sweep(time_a, time_b, 3, tall - 3, 1)
-    for k in range(group):
+
+    def send_times(k):
         for i in range(n_space):
             q = (p + i) % n_space
             piece = time_b.at[k, inner, q, :]
@@ -366,14 +419,7 @@
                 def _():
                     send()
 
-    def source_row(i, carry):
-        at = pl.ds(pl.multiple_of(i * n_space, n_space), n_space)
-        for k in range(group):
-            shift = time_b[k, i + 4] - start[k, i + 4]
-            source[k, i] = count[at, :] * shift - late[k, at, :]
-        return carry
-
-    lax.fori_loop(0, src_rows, source_row, 0, unroll=2)
+    send_times(0)
 
     def weight_row(i, carry):
         j = i + 5
@@ -398,6 +444,19 @@
 
     lax.fori_loop(0, src_rows - 2, weight_row, 0, unroll=4)
 
+    events_before.wait_recv()
+    events_after.wait_recv()
+
+    def source_row(i, carry):
+        valid = row_valid(y_base - 5 + i)
+        for k in range(group):
+            shift = time_b[k, i + 4] - start[k, i + 4]
+            value = landed[i, 0] * shift - landed[i, 1 + k]
+            source[k, i] = jnp.where(valid, value, 0.0)
+        return carry
+
+    lax.fori_loop(0, src_rows, source_row, 0, unroll=2)
+
     def adjoint_sweep(old, new, low, high):
         def row(i, carry):
             for k in range(group):
@@ -455,6 +514,8 @@
                 device_id=(q * group + g, p),
                 device_id_type=MESH,
             ).start()
+    for k in range(1, group):
+        send_times(k)
     pltpu.make_async_copy(parts, parts, recv_sem.at[7]).wait()
     summed = parts[0]
     for i in range(1, peers):
@@ -492,8 +553,10 @@
     for _ in partners:
         drain(delay.at[0], send_sem.at[2])
         drain(meta.at[0], send_sem.at[3])
-    to_before.wait_send()
-    to_after.wait_send()
+    for halo in halos:
+        halo.wait_send()
+    events_before.wait_send()
+    events_after.wait_send()
     drain(times_out.at[pl.ds(0, (n_blocks - 1) * rows), :], send_sem.at[6])
     drain(parts.at[pl.ds(1, peers - 1)], send_sem.at[7])
     for k in range(chunk_x):
@@ -516,20 +579,9 @@
     chunk_x = n_space // peers
     own_rows = ny // n_src
     src_rows = rows + 10
-    flags = active.reshape(1, -1).astype(jnp.float32)
-    cells = station_cells.astype(jnp.float32)
-    meta = jnp.concatenate(
-        [
-            flags,
-            jnp.zeros((1, 64 - flags.shape[1]), jnp.float32),
-            cells,
-            jnp.zeros((1, 61), jnp.float32),
-        ],
-        axis=1,
-    )
     f32 = jnp.float32
     plane = (n_space, nz)
-    vmem = pl.BlockSpec(memory_space=pltpu.VMEM)
+    smem = pl.BlockSpec(memory_space=pltpu.SMEM)
     anywhere = pl.BlockSpec(memory_space=pl.ANY)
     hbm = pl.BlockSpec(memory_space=pltpu.HBM)
     times, kernel_part = pl.pallas_call(
@@ -538,9 +590,10 @@
             jax.ShapeDtypeStruct((ny, nz), f32),
             jax.ShapeDtypeStruct((own_rows, nz), f32),
         ),
-        in_specs=[hbm, vmem, hbm, hbm],
+        in_specs=[hbm, smem, smem, hbm, hbm],
         out_specs=(anywhere, anywhere),
         scratch_shapes=[
+            pltpu.VMEM((1, 128), f32),
             pltpu.VMEM((3, events), jnp.int32),
             pltpu.VMEM((tall,) + plane, f32),
             pltpu.VMEM((tall,) + plane, f32),
@@ -549,8 +602,7 @@
             pltpu.VMEM((GROUP, tall + 2) + plane, f32),
             pltpu.VMEM((GROUP, tall + 2) + plane, f32),
             pltpu.VMEM((GROUP, tall + 2) + plane, f32),
-            pltpu.VMEM((src_rows * n_space, nz), f32),
-            pltpu.VMEM((GROUP, src_rows * n_space, nz), f32),
+            pltpu.VMEM((src_rows, 1 + GROUP) + plane, f32),
             pltpu.VMEM((2, GROUP, 3) + plane, f32),
             pltpu.VMEM((GROUP,) + plane, f32),
             pltpu.VMEM((GROUP, 6, src_rows - 2) + plane, f32),
@@ -563,13 +615,15 @@
             pltpu.VMEM((rows, chunk_x, nz), f32),
             pltpu.SemaphoreType.DMA,
             pltpu.SemaphoreType.DMA((8,)),
-            pltpu.SemaphoreType.DMA((9,)),
+            pltpu.SemaphoreType.DMA((10,)),
+            pltpu.SemaphoreType.DMA((4,)),
+            pltpu.SemaphoreType.DMA((4,)),
             pltpu.SemaphoreType.DMA((chunk_x,)),
         ],
         compiler_params=pltpu.CompilerParams(
             collective_id=0, has_side_effects=True, vmem_limit_bytes=60 << 20
         ),
-    )(velocity[0], meta, event_cells, delays)
+    )(velocity[0], station_cells, active[:, 0, 0, :], event_cells, delays)
     return times[None, None], kernel_part[None]
 
 

time: 72.1 us -> 66.9 us (0.928)
  the two profiles are of different devices: /device:TPU:7 before, /device:TPU:15 now
where the time goes in v3:
time: 66.9 us; the launch traced here: 66.7 us
  Pallas kernels  63.6 us (95%)
  local copies, waits for them, and re-layouts  2.49 us (4%)
    pallas_call x1, Pallas kernels, per_device(): pl.pallas_call(functools.partial(kernel, dims), out_shape=(jax.ShapeDtype...  63.6 us
    unnamed x4, local copies, waits for them, and re-layouts  2.49 us

profile of v3, /device:TPU:15, one launch (start us, length us, event | category | flops | bytes accessed | tf_op | source)
XLA Modules:
  0.0 66.7 jit_solution(6491735559013191434)
XLA Ops:
  0.6 63.6 %shard_map.68 = (f32[512,256]{1,0:T(8,128)}, f32[32,256]{1,0:T(8,128)}) custom-call(f32[512,256]{1,0:T(8,128)} %bitcast.4, s32[1,3]{1,0:T(1,128)} %cells_ref.1, s32[2,16]{1,0:T(2,128)} %bitcast.7, s32[3,8192]{1,0:T(4,128)} %events_hbm.1, f32[1,8192]{1,0:T(1,128)} %delays_ref.1), custom_call_target="tpu_custom_call" | custom-call | tf_op jit(solution)/shard_map/pallas_call | solution.py:587
  64.2 0.0 copy-start
  64.2 1.9 %copy.9 = f32[1,1,512,256]{3,2,1,0:T(8,128)} copy(f32[1,1,512,256]{3,2,1,0:T(8,128)} %bitcast.5) | data formatting | bytes 1048576
  66.1 0.0 copy-done
  66.1 0.6 copy.10
Async XLA Ops:
  64.2 1.9 %copy-start = (f32[32,256]{1,0:T(8,128)S(1)}, f32[32,256]{1,0:T(8,128)}, u32[]{:S(2)}) copy-start(f32[32,256]{1,0:T(8,128)} %get-tuple-element.5) | copy-start | bytes 98308

commit v4 on v3

--- a/solution.py
+++ b/solution.py
@@ -14,27 +14,22 @@
 MESH = pl.DeviceIdType.MESH
 
 
-def godunov(near_x, near_y, near_z, cost):
+def godunov(near_x, near_y, near_z, cost, cost_1, cost_2, cost_3):
     low_xy = jnp.minimum(near_x, near_y)
     high_xy = jnp.maximum(near_x, near_y)
     lowest = jnp.minimum(low_xy, near_z)
     rest = jnp.maximum(low_xy, near_z)
-    middle = jnp.minimum(high_xy, rest)
-    highest = jnp.maximum(high_xy, rest)
-    gap2 = middle - lowest
-    gap3 = highest - lowest
-    cost_sq = cost * cost
-    gap2_sq = gap2 * gap2
-    disc2 = 2.0 * cost_sq - gap2_sq
-    reach = gap3 + gap3 - gap2
-    two = disc2 <= reach * reach
+    gap2 = jnp.minimum(high_xy, rest) - lowest
+    gap3 = jnp.maximum(high_xy, rest) - lowest
     step = gap3 - gap2
-    disc3 = 3.0 * cost_sq - (gap2_sq + gap3 * gap3 + step * step)
-    disc = jnp.where(two, disc2, disc3)
-    base = jnp.where(two, gap2, gap2 + gap3)
+    spread = gap3 * gap3 + step * step
+    two = cost_1 <= spread
+    disc = jnp.where(two, cost_2, cost_3 - spread) - gap2 * gap2
+    base = gap2 + jnp.where(two, 0.0, gap3)
     scale = jnp.where(two, 0.5, 1.0 / 3.0)
-    wide = lowest + (base + root(jnp.maximum(disc, 1e-30))) * scale
-    return jnp.where(cost <= gap2, lowest + cost, wide)
+    disc = jnp.maximum(disc, 1e-30)
+    wide = (base + disc * lax.rsqrt(disc)) * scale
+    return lowest + jnp.where(cost <= gap2, cost, wide)
 
 
 def tiles_of(ref, index):
@@ -346,22 +341,28 @@
     def sweep_row(old, new, r, j):
         y = y_base - HALO + j
         kind = jnp.where(row_valid(y), (y + TY) // TY - 1 - first_tile, 2)
-        for k in range(group):
-            centre = tiles_of(old, (k, j + 1))
-            x_low, x_high = beside_x(centre, BIG)
-            z_low, z_high = beside_z(centre, BIG)
-            for t, h in centre:
-                tile = at_tile(t, h)
+        level = y.astype(jnp.float32)
+        centre = [tiles_of(old, (k, j + 1)) for k in range(group)]
+        near_x = [beside_x(field, BIG) for field in centre]
+        near_z = [beside_z(field, BIG) for field in centre]
+        for t, h in centre[0]:
+            tile = at_tile(t, h)
+            cost = slow[(j,) + tile]
+            cost_1 = cost * cost
+            cost_2 = cost_1 + cost_1
+            cost_3 = cost_2 + cost_1
+            for k in range(group):
                 update = godunov(
-                    jnp.minimum(x_low[t, h], x_high[t, h]),
+                    jnp.minimum(near_x[k][0][t, h], near_x[k][1][t, h]),
                     jnp.minimum(old[(k, j) + tile], old[(k, j + 2) + tile]),
-                    jnp.minimum(z_low[t, h], z_high[t, h]),
-                    slow[(j,) + tile],
+                    jnp.minimum(near_z[k][0][t, h], near_z[k][1][t, h]),
+                    cost,
+                    cost_1,
+                    cost_2,
+                    cost_3,
                 )
-                chosen = (masks[(r, k, kind) + tile] > 0.0) & (
-                    spot[(k,) + tile] != y.astype(jnp.float32)
-                )
-                new[(k, j + 1) + tile] = jnp.where(chosen, update, centre[t, h])
+                chosen = (masks[(r, k, kind) + tile] > 0.0) & (spot[(k,) + tile] != level)
+                new[(k, j + 1) + tile] = jnp.where(chosen, update, centre[k][t, h])
 
     stages = ((start, time_a, 0), (time_a, time_b, 0), (time_b, time_a, 1), (time_a, time_b, 1))
     lax.fori_loop(HALO, HALO + rows, slow_row, 0, unroll=4)
@@ -621,9 +622,14 @@
             pltpu.SemaphoreType.DMA((chunk_x,)),
         ],
         compiler_params=pltpu.CompilerParams(
-            collective_id=0, has_side_effects=True, vmem_limit_bytes=60 << 20
+            collective_id=0, has_side_effects=True, vmem_limit_bytes=48 << 20
         ),
-    )(velocity[0], station_cells, active[:, 0, 0, :], event_cells, delays)
+    )(
+        *(
+            pltpu.with_memory_space_constraint(array, pltpu.HBM)
+            for array in (velocity[0], station_cells, active[:, 0, 0, :], event_cells, delays)
+        )
+    )
     return times[None, None], kernel_part[None]
 
 

time: 66.9 us -> 67.4 us (level)
  the two profiles are of different devices: /device:TPU:15 before, /device:TPU:3 now
where the time goes in v4:
time: 67.4 us; the launch traced here: 67.3 us
  Pallas kernels  65.2 us (97%)
  local copies, waits for them, and re-layouts  1.41 us (2%)
    pallas_call x1, Pallas kernels, per_device(): pl.pallas_call(functools.partial(kernel, dims), out_shape=(jax.ShapeDtype...  65.2 us
    unnamed x2, local copies, waits for them, and re-layouts  1.41 us

profile of v4, /device:TPU:3, one launch (start us, length us, event | category | flops | bytes accessed | tf_op | source)
XLA Modules:
  0.0 67.3 jit_solution(4400330202053515106)
XLA Ops:
  0.6 65.2 %shard_map.68 = (f32[512,256]{1,0:T(8,128)S(1)}, f32[32,256]{1,0:T(8,128)S(1)}) custom-call(f32[512,256]{1,0:T(8,128)} %bitcast.6, s32[1,3]{1,0:T(1,128)} %cells_ref.1, s32[2,16]{1,0:T(2,128)} %bitcast.7, s32[3,8192]{1,0:T(4,128)} %events_hbm.1, f32[1,8192]{1,0:T(1,128)} %delays_ref.1), custom_call_target="tpu_custom_call" | custom-call | tf_op jit(solution)/shard_map/pallas_call | solution.py:588
  65.9 0.8 %copy.9 = f32[1,1,512,256]{3,2,1,0:T(8,128)} copy(f32[1,1,512,256]{3,2,1,0:T(8,128)S(1)} %bitcast.4) | data formatting | bytes 1048576
  66.6 0.6 copy.10

commit v5 on v4

--- a/solution.py
+++ b/solution.py
@@ -84,7 +84,9 @@
     start,
     time_a,
     time_b,
+    count,
     landed,
+    left,
     masks,
     spot,
     weights,
@@ -100,6 +102,8 @@
     recv_sem,
     halo_send,
     halo_recv,
+    event_send,
+    event_recv,
     last_sem,
 ):
     n_src, n_space, ny, nz, events = dims
@@ -162,6 +166,34 @@
             pl.semaphore_signal(barrier, inc=1, device_id=to, device_id_type=MESH)
 
         signals = signals + jnp.where(mine, 0, 1)
+
+    src_rows = rows + 10
+    cells = rows * n_space
+    step_events = 2048
+    steps = events // step_events
+    contract = (((1,), (1,)), ((), ()))
+    mine_rows = pl.ds(5, rows)
+    count[mine_rows] = jnp.zeros((rows, n_space, nz), jnp.float32)
+    fetch_events.wait()
+
+    def product(first, second):
+        out = lax.dot_general(first, second, contract, preferred_element_type=jnp.float32)
+        return out.reshape(rows, n_space, nz)
+
+    def depth_of(at):
+        deep = lax.broadcasted_iota(jnp.int32, (nz, step_events), 0)
+        return deep == events_ref[2:3, at]
+
+    def count_events(c, carry):
+        at = pl.ds(pl.multiple_of(c * step_events, step_events), step_events)
+        key = (events_ref[1:2, at] - y_base) * n_space + events_ref[0:1, at]
+        cell = lax.broadcasted_iota(jnp.int32, (cells, step_events), 0)
+        left[:, at] = jnp.where(cell == key, 1.0, 0.0).astype(jnp.bfloat16)
+        right = jnp.where(depth_of(at), 1.0, 0.0).astype(jnp.bfloat16)
+        count[mine_rows] += product(left[:, at], right)
+        return carry
+
+    lax.fori_loop(0, steps, count_events, 0)
     pl.semaphore_wait(barrier, signals)
 
     own = pl.ds(HALO, rows)
@@ -212,36 +244,36 @@
             device_id_type=MESH,
         ).start()
 
-    src_rows = rows + 10
-    cells = rows * n_space
-    step_events = 1024
-    steps = events // step_events
-    mine_rows = pl.ds(5, rows)
-    landed[mine_rows] = jnp.zeros((rows, 1 + group, n_space, nz), jnp.float32)
-    fetch_events.wait()
+    before = where_is((block + n_blocks - 1) % n_blocks)
+    after = where_is((block + 1) % n_blocks)
+
+    def event_halo(ref, n, to):
+        at, there = ((5, 5 + rows), (rows, 0))[n % 2]
+        return pltpu.make_async_remote_copy(
+            ref.at[pl.ds(at, 5)],
+            ref.at[pl.ds(there, 5)],
+            event_send.at[n],
+            event_recv.at[n],
+            device_id=to,
+            device_id_type=MESH,
+        )
+
     pltpu.make_async_copy(delay, delay, recv_sem.at[2]).wait()
+    event_halos = [event_halo(count, 0, before), event_halo(count, 1, after)]
+    for halo in event_halos:
+        halo.start()
+
+    landed[mine_rows] = jnp.zeros((rows, group, n_space, nz), jnp.float32)
 
     def add_events(c, carry):
         at = pl.ds(pl.multiple_of(c * step_events, step_events), step_events)
-        event_x = events_ref[0:1, at]
-        event_y = events_ref[1:2, at]
-        event_z = events_ref[2:3, at]
-        key = (event_y - y_base) * n_space + event_x
-        cell = lax.broadcasted_iota(jnp.int32, (cells, step_events), 0)
-        left = jnp.where(cell == key, 1.0, 0.0).astype(jnp.bfloat16)
-        deep = lax.broadcasted_iota(jnp.int32, (nz, step_events), 0) == event_z
-        contract = (((1,), (1,)), ((), ()))
-
-        def product(value):
-            right = jnp.where(deep, value, 0.0).astype(jnp.bfloat16)
-            out = lax.dot_general(left, right, contract, preferred_element_type=jnp.float32)
-            return out.reshape(rows, n_space, nz)
-
-        landed[mine_rows, 0] += product(1.0)
+        deep = depth_of(at)
         for k in range(group):
             lateness = delay[k, 0:1, at]
             coarse = lateness.astype(jnp.bfloat16).astype(jnp.float32)
-            landed[mine_rows, 1 + k] += product(coarse) + product(lateness - coarse)
+            for value in (coarse, lateness - coarse):
+                right = jnp.where(deep, value, 0.0).astype(jnp.bfloat16)
+                landed[mine_rows, k] += product(left[:, at], right)
         return carry
 
     wide_lane = lax.broadcasted_iota(jnp.int32, (n_space, 128), 1)
@@ -279,8 +311,6 @@
 
             lax.fori_loop(0, tall + 2, init_row, 0, unroll=2)
 
-    before = where_is((block + n_blocks - 1) % n_blocks)
-    after = where_is((block + 1) % n_blocks)
     cut = steps // 2
     lax.fori_loop(0, cut, add_events, 0)
 
@@ -317,22 +347,10 @@
         if n == 0:
             init_fields()
 
-    events_before = pltpu.make_async_remote_copy(
-        landed.at[pl.ds(5, 5)],
-        landed.at[pl.ds(5 + rows, 5)],
-        send_sem.at[4],
-        recv_sem.at[4],
-        device_id=before,
-        device_id_type=MESH,
-    )
-    events_after = pltpu.make_async_remote_copy(
-        landed.at[pl.ds(rows, 5)],
-        landed.at[pl.ds(0, 5)],
-        send_sem.at[5],
-        recv_sem.at[5],
-        device_id=after,
-        device_id_type=MESH,
-    )
+    for n, to in ((2, before), (3, after)):
+        halo = event_halo(landed, n, to)
+        halo.start()
+        event_halos.append(halo)
 
     def slow_row(j, carry):
         slow[j] = 1.0 / vel[j]
@@ -376,8 +394,6 @@
 
     for halo in halos:
         halo.wait_recv()
-    events_before.start()
-    events_after.start()
     lax.fori_loop(0, HALO, slow_row, 0, unroll=4)
     lax.fori_loop(HALO + rows, tall, slow_row, 0, unroll=4)
     for n, (old, new, r) in enumerate(stages):
@@ -387,7 +403,7 @@
             sweep_row(old, new, r, HALO + rows - n + i)
             return carry
 
-        lax.fori_loop(0, HALO, outside, 0, unroll=2)
+        lax.fori_loop(0, HALO, outside, 0, unroll=4)
 
     inner = pl.ds(HALO + 1, rows)
 
@@ -445,14 +461,14 @@
 
     lax.fori_loop(0, src_rows - 2, weight_row, 0, unroll=4)
 
-    events_before.wait_recv()
-    events_after.wait_recv()
+    for halo in event_halos:
+        halo.wait_recv()
 
     def source_row(i, carry):
         valid = row_valid(y_base - 5 + i)
         for k in range(group):
             shift = time_b[k, i + 4] - start[k, i + 4]
-            value = landed[i, 0] * shift - landed[i, 1 + k]
+            value = count[i] * shift - landed[i, k]
             source[k, i] = jnp.where(valid, value, 0.0)
         return carry
 
@@ -556,8 +572,8 @@
         drain(meta.at[0], send_sem.at[3])
     for halo in halos:
         halo.wait_send()
-    events_before.wait_send()
-    events_after.wait_send()
+    for halo in event_halos:
+        halo.wait_send()
     drain(times_out.at[pl.ds(0, (n_blocks - 1) * rows), :], send_sem.at[6])
     drain(parts.at[pl.ds(1, peers - 1)], send_sem.at[7])
     for k in range(chunk_x):
@@ -603,7 +619,9 @@
             pltpu.VMEM((GROUP, tall + 2) + plane, f32),
             pltpu.VMEM((GROUP, tall + 2) + plane, f32),
             pltpu.VMEM((GROUP, tall + 2) + plane, f32),
-            pltpu.VMEM((src_rows, 1 + GROUP) + plane, f32),
+            pltpu.VMEM((src_rows,) + plane, f32),
+            pltpu.VMEM((src_rows, GROUP) + plane, f32),
+            pltpu.VMEM((rows * n_space, events), jnp.bfloat16),
             pltpu.VMEM((2, GROUP, 3) + plane, f32),
             pltpu.VMEM((GROUP,) + plane, f32),
             pltpu.VMEM((GROUP, 6, src_rows - 2) + plane, f32),
@@ -619,6 +637,8 @@
             pltpu.SemaphoreType.DMA((10,)),
             pltpu.SemaphoreType.DMA((4,)),
             pltpu.SemaphoreType.DMA((4,)),
+            pltpu.SemaphoreType.DMA((4,)),
+            pltpu.SemaphoreType.DMA((4,)),
             pltpu.SemaphoreType.DMA((chunk_x,)),
         ],
         compiler_params=pltpu.CompilerParams(

time: 67.4 us -> 64.1 us (0.951)
  the two profiles are of different devices: /device:TPU:3 before, /device:TPU:31 now
where the time goes in v5:
time: 64.1 us; the launch traced here: 63.9 us
  Pallas kernels  61.8 us (96%)
  local copies, waits for them, and re-layouts  1.41 us (2%)
    pallas_call x1, Pallas kernels, per_device(): pl.pallas_call(functools.partial(kernel, dims), out_shape=(jax.ShapeDtype...  61.8 us
    unnamed x2, local copies, waits for them, and re-layouts  1.41 us

profile of v5, /device:TPU:31, one launch (start us, length us, event | category | flops | bytes accessed | tf_op | source)
XLA Modules:
  0.0 63.9 jit_solution(2497909866471439491)
XLA Ops:
  0.6 61.8 %shard_map.68 = (f32[512,256]{1,0:T(8,128)S(1)}, f32[32,256]{1,0:T(8,128)S(1)}) custom-call(f32[512,256]{1,0:T(8,128)} %bitcast.6, s32[1,3]{1,0:T(1,128)} %cells_ref.1, s32[2,16]{1,0:T(2,128)} %bitcast.7, s32[3,8192]{1,0:T(4,128)} %events_hbm.1, f32[1,8192]{1,0:T(1,128)} %delays_ref.1), custom_call_target="tpu_custom_call" | custom-call | tf_op jit(solution)/shard_map/pallas_call | solution.py:604
  62.5 0.8 %copy.9 = f32[1,1,512,256]{3,2,1,0:T(8,128)} copy(f32[1,1,512,256]{3,2,1,0:T(8,128)S(1)} %bitcast.4) | data formatting | bytes 1048576
  63.2 0.6 copy.10

commit v6 on v5

--- a/solution.py
+++ b/solution.py
@@ -169,7 +169,7 @@
 
     src_rows = rows + 10
     cells = rows * n_space
-    step_events = 2048
+    step_events = 4096
     steps = events // step_events
     contract = (((1,), (1,)), ((), ()))
     mine_rows = pl.ds(5, rows)
@@ -271,9 +271,11 @@
         for k in range(group):
             lateness = delay[k, 0:1, at]
             coarse = lateness.astype(jnp.bfloat16).astype(jnp.float32)
-            for value in (coarse, lateness - coarse):
-                right = jnp.where(deep, value, 0.0).astype(jnp.bfloat16)
-                landed[mine_rows, k] += product(left[:, at], right)
+            sums = [
+                product(left[:, at], jnp.where(deep, value, 0.0).astype(jnp.bfloat16))
+                for value in (coarse, lateness - coarse)
+            ]
+            landed[mine_rows, k] += sums[0] + sums[1]
         return carry
 
     wide_lane = lax.broadcasted_iota(jnp.int32, (n_space, 128), 1)
@@ -309,7 +311,7 @@
                 start[k, j] = jnp.where(row_valid(y), root(flat + diff * diff), BIG)
                 return carry
 
-            lax.fori_loop(0, tall + 2, init_row, 0, unroll=2)
+            lax.fori_loop(0, tall + 2, init_row, 0, unroll=4)
 
     cut = steps // 2
     lax.fori_loop(0, cut, add_events, 0)
@@ -344,13 +346,13 @@
             )
             halo.start()
             halos.append(halo)
-        if n == 0:
-            init_fields()
 
     for n, to in ((2, before), (3, after)):
         halo = event_halo(landed, n, to)
         halo.start()
         event_halos.append(halo)
+
+    init_fields()
 
     def slow_row(j, carry):
         slow[j] = 1.0 / vel[j]

time: 64.1 us -> 60.7 us (0.947)
  Pallas kernels: 61.8 us -> 58.5 us
    pallas_call x1, Pallas kernels: 61.8 us -> 58.5 us  [per_device(): pl.pallas_call(functools.partial(kernel, dims), out_shape=(jax.ShapeDtype...]
where the time goes in v6:
time: 60.7 us; the launch traced here: 60.5 us
  Pallas kernels  58.5 us (96%)
  local copies, waits for them, and re-layouts  1.41 us (2%)
  between operations  0.64 us (1%)
    pallas_call x1, Pallas kernels, per_device(): pl.pallas_call(functools.partial(kernel, dims), out_shape=(jax.ShapeDtype...  58.5 us
    unnamed x2, local copies, waits for them, and re-layouts  1.41 us

profile of v6, /device:TPU:31, one launch (start us, length us, event | category | flops | bytes accessed | tf_op | source)
XLA Modules:
  0.0 60.5 jit_solution(389294219128300706)
XLA Ops:
  0.6 58.5 %shard_map.68 = (f32[512,256]{1,0:T(8,128)S(1)}, f32[32,256]{1,0:T(8,128)S(1)}) custom-call(f32[512,256]{1,0:T(8,128)} %bitcast.6, s32[1,3]{1,0:T(1,128)} %cells_ref.1, s32[2,16]{1,0:T(2,128)} %bitcast.7, s32[3,8192]{1,0:T(4,128)} %events_hbm.1, f32[1,8192]{1,0:T(1,128)} %delays_ref.1), custom_call_target="tpu_custom_call" | custom-call | tf_op jit(solution)/shard_map/pallas_call | solution.py:606
  59.1 0.8 %copy.9 = f32[1,1,512,256]{3,2,1,0:T(8,128)} copy(f32[1,1,512,256]{3,2,1,0:T(8,128)S(1)} %bitcast.4) | data formatting | bytes 1048576
  59.9 0.6 %copy.10 = f32[1,32,256]{2,1,0:T(8,128)} copy(f32[1,32,256]{2,1,0:T(8,128)S(1)} %bitcast.5) | data formatting | bytes 65536
